TPU v7x, 32 devices: a whole 2x2x4 slice. The times are simulated.
32 devices in a mesh: groups: 2 (over y), win: 4 (over z), head: 2 (over x), sub: 2 (over core).
Axes of the slice: x: 2, y: 2, z: 4, core: 2. Of those that a mesh axis runs over, the one named last changes fastest.
Arguments:
- queries: float32 [2048, 6144], P(('groups', 'win'), ('head', 'sub')), parts along dimension 0, may hold values from -6.5 to 6.5
- key_rows: float32 [2048, 6144], P(('groups', 'win'), ('head', 'sub')), parts along dimension 0, may hold values from -6.5 to 6.5
- value_rows: float32 [2048, 6144], P(('groups', 'win'), ('head', 'sub')), parts along dimension 0, may hold values from -6 to 6
- merge_target: int32 [2048], P(('groups', 'win')), parts along dimension 0, may hold values from 0 to 831, as said below
Outputs:
- attended: float32 [2048, 6144], P(('groups', 'win'), ('head', 'sub')), parts along dimension 0
There are 2 independent parts, one for each index of `groups`. A program takes and returns all parts, laid end to end along the dimension named above; each array names one. Nothing has to cross between parts.
Inputs may be any that keep to these rules, and one draw needn't show every extreme that they name: merge_target[r] lies in window merge_target[r] // 208; every merged row is joined by one or more rows; of the rows of one window, at most 64 join merged rows of any one window, exactly 64 join those of some window, and at least 52 join those of every window.
All inputs are finite; a program needn't handle non-finite values.
Results may differ from a plain program's by a relative error of at most 0.0003.
Values sent between devices are 32-bit elements; how exact they have to be, the bound alone decides.
No kernel may reach another device: no remote copies, remote signals or barrier semaphores. Data moves between devices by JAX's collectives and lax.ppermute only.
A program may use at most 64 MiB of HBM per device.

v0:
```python
import functools
import math

import jax
import jax.numpy as jnp
from jax import lax
from jax.experimental import pallas as pl
from jax.experimental.pallas import tpu as pltpu
from jax.sharding import PartitionSpec as P


HEAD_DIM = 128
ROWS_PER_WINDOW = 256
MERGED_WINDOW_ROWS = 208


def slot_layout(merge_target, window_count, capacity):
    target_window = merge_target // MERGED_WINDOW_ROWS
    target_place = merge_target % MERGED_WINDOW_ROWS
    member = (target_window[:, None] == jnp.arange(window_count, dtype=jnp.int32)[None, :]).astype(
        jnp.int32
    )
    earlier = jnp.cumsum(member, axis=0) - member
    position = jnp.sum(earlier * member, axis=1)
    slot_index = target_window * capacity + position
    slot_total = window_count * capacity
    row_count = merge_target.shape[0]
    source_row = (
        jnp.full((slot_total,), row_count, jnp.int32)
        .at[slot_index]
        .set(jnp.arange(row_count, dtype=jnp.int32))
    )
    labels_flat = (
        jnp.zeros((slot_total,), jnp.float32)
        .at[slot_index]
        .set((target_place + 1).astype(jnp.float32))
    )
    return (slot_index, source_row, labels_flat.reshape(window_count, capacity))


def pack_rows(source, source_row, window_count, capacity):
    padding = jnp.zeros((1, source.shape[1]), source.dtype)
    return jnp.concatenate([source, padding], 0)[source_row].reshape(
        window_count, capacity, source.shape[1]
    )


def slot_counts(labels):
    label_index = labels.reshape(-1).astype(jnp.int32) - 1
    segment = jnp.where(label_index < 0, MERGED_WINDOW_ROWS, label_index)
    counts = jax.ops.segment_sum(
        jnp.ones(segment.shape, jnp.float32), segment, MERGED_WINDOW_ROWS + 1
    )[:MERGED_WINDOW_ROWS]
    return (segment, counts)


def average_slots(received, segment, counts):
    flattened = received.reshape(-1, received.shape[-1])
    totals = jax.ops.segment_sum(flattened, segment, MERGED_WINDOW_ROWS + 1)[:MERGED_WINDOW_ROWS]
    return totals / counts[:, None]


def by_windows(queries, key_rows, value_rows, merge_target):
    window_count = lax.axis_size("win")
    capacity = MERGED_WINDOW_ROWS // window_count + (ROWS_PER_WINDOW - MERGED_WINDOW_ROWS) // 4
    col_width = queries.shape[1]
    head_count = col_width // HEAD_DIM
    slot_index, source_row, labels = slot_layout(merge_target, window_count, capacity)
    pair_rows = jnp.concatenate([key_rows, value_rows], 1)
    packed_pair = pack_rows(pair_rows, source_row, window_count, capacity)
    received_pair, got_labels = (
        lax.all_to_all(packed_pair, "win", split_axis=0, concat_axis=0, tiled=True),
        lax.all_to_all(labels, "win", split_axis=0, concat_axis=0, tiled=True),
    )
    segment, counts = slot_counts(got_labels)
    merged_pair = average_slots(received_pair, segment, counts)
    merged_keys = merged_pair[:, :col_width]
    merged_values = merged_pair[:, col_width:]
    packed_queries = pack_rows(queries, source_row, window_count, capacity)
    received_queries = lax.all_to_all(
        packed_queries, "win", split_axis=0, concat_axis=0, tiled=True
    )
    merged_queries = average_slots(received_queries, segment, counts)
    scaling = 1.0 / math.sqrt(HEAD_DIM)
    query_head_stack = merged_queries.reshape(MERGED_WINDOW_ROWS, head_count, HEAD_DIM)
    running_max = jnp.full((head_count, MERGED_WINDOW_ROWS), -1e30, jnp.float32)
    portion_keys = lax.all_gather(merged_keys, "win", axis=0, tiled=True)
    portion_values = lax.all_gather(merged_values, "win", axis=0, tiled=True)
    key_head_stack = portion_keys.reshape(-1, head_count, HEAD_DIM)
    value_head_stack = portion_values.reshape(-1, head_count, HEAD_DIM)
    scores = (
        jnp.einsum(
            "frk,grk->rfg", query_head_stack, key_head_stack, precision=lax.Precision.HIGHEST
        )
        * scaling
    )
    new_max = jnp.maximum(running_max, jnp.max(scores, axis=2))
    attention_weight = jnp.exp(scores - new_max[:, :, None])
    new_sum = jnp.sum(attention_weight, axis=2)
    appended_rows = jnp.einsum(
        "tak,ktl->atl", attention_weight, value_head_stack, precision=lax.Precision.HIGHEST
    )
    merged_output = (appended_rows / jnp.transpose(new_sum)[:, :, None]).reshape(
        MERGED_WINDOW_ROWS, col_width
    )
    padded_output = jnp.concatenate([merged_output, jnp.zeros((1, col_width), jnp.float32)], 0)
    outgoing = padded_output[segment].reshape(window_count, capacity, col_width)
    returned = lax.all_to_all(outgoing, "win", split_axis=0, concat_axis=0, tiled=True)
    return returned.reshape(-1, col_width)[slot_index]


def split_terms(x):
    high = x.astype(jnp.bfloat16)
    low = (x - high.astype(jnp.float32)).astype(jnp.bfloat16)
    return high, low


def pack_kernel(flip, head, per_window, tailed, *refs):
    sources = refs[:3]
    packed_ref, landed = refs[3 + tailed], refs[4 + tailed]
    rows = sources[0].shape[0]
    peer = lax.axis_index("win") ^ flip
    first = pl.multiple_of((peer * per_window + head) * HEAD_DIM, HEAD_DIM)
    copies = [
        pltpu.make_async_copy(
            source.at[:, pl.ds(first, HEAD_DIM)],
            packed_ref.at[pl.ds(part * rows, rows), :],
            landed.at[part],
        )
        for part, source in enumerate(sources)
    ]
    if tailed:
        places_ref = refs[-1]
        copies.insert(0, pltpu.make_async_copy(refs[3], places_ref, landed.at[3]))
    for copy in copies:
        copy.start()
    for copy in copies:
        copy.wait()
    if tailed:
        lines = rows // HEAD_DIM
        packed_ref[3 * rows : 3 * rows + lines, :] = places_ref[...].astype(jnp.float32)
        packed_ref[3 * rows + lines :, :] = jnp.zeros((8 - lines, HEAD_DIM), jnp.float32)


def pack(sources, flip, head, per_window, places=None):
    rows = sources[0].shape[0]
    tailed = places is not None
    total = 3 * rows + 8 * tailed
    extra = [places] if tailed else []
    return pl.pallas_call(
        functools.partial(pack_kernel, flip, head, per_window, tailed),
        in_specs=[pl.BlockSpec(memory_space=pl.ANY)] * (3 + tailed),
        out_specs=pl.BlockSpec(memory_space=pltpu.VMEM),
        out_shape=jax.ShapeDtypeStruct((total, HEAD_DIM), jnp.float32),
        scratch_shapes=[pltpu.SemaphoreType.DMA((3 + tailed,))]
        + [pltpu.VMEM(p.shape, p.dtype) for p in extra],
        cost_estimate=pl.CostEstimate(
            flops=0, transcendentals=0, bytes_accessed=8 * total * HEAD_DIM
        ),
        name="pack",
    )(*sources, *extra)


def place_kernel(head, per_window, peers, *refs):
    blocks = refs[:len(peers)]
    result_ref, landed = refs[-2:]
    copies = []
    for n, (block, flip) in enumerate(zip(blocks, peers)):
        peer = lax.axis_index("win") ^ flip
        first = pl.multiple_of((peer * per_window + head[n]) * HEAD_DIM, HEAD_DIM)
        copies.append(
            pltpu.make_async_copy(block, result_ref.at[:, pl.ds(first, HEAD_DIM)], landed.at[n])
        )
    for copy in copies:
        copy.start()
    for copy in copies:
        copy.wait()


def put_blocks(entries, per_window, result_shape, result=None):
    blocks = [entry[2] for entry in entries]
    flips, heads = [entry[0] for entry in entries], [entry[1] for entry in entries]
    anywhere = pl.BlockSpec(memory_space=pl.ANY)
    extra = [] if result is None else [result]
    return pl.pallas_call(
        functools.partial(place_kernel, heads, per_window, flips),
        in_specs=[pl.BlockSpec(memory_space=pltpu.VMEM)] * len(blocks) + [anywhere] * len(extra),
        out_specs=anywhere,
        out_shape=result_shape,
        input_output_aliases={len(blocks): 0} if extra else {},
        scratch_shapes=[pltpu.SemaphoreType.DMA((len(blocks),))],
        cost_estimate=pl.CostEstimate(
            flops=0, transcendentals=0, bytes_accessed=8 * blocks[0].size * len(blocks)
        ),
        name="put_blocks",
    )(*blocks, *extra)


def attend_kernel(peers, place_row_ref, place_col_ref, *refs):
    received, returned = refs[:peers], refs[peers : 2 * peers]
    rows_ref, query_cat, key_high, key_low, value_cat, output_cat = refs[2 * peers :]
    rows = returned[0].shape[0]
    row_total = rows * peers
    merged_total = query_cat.shape[0]
    tile = MERGED_WINDOW_ROWS

    for part in range(3):
        for piece in range(peers):
            high, low = split_terms(received[piece][part * rows : (part + 1) * rows, :])
            span = slice(piece * rows, (piece + 1) * rows)
            rows_ref[span, 2 * part * HEAD_DIM : (2 * part + 1) * HEAD_DIM] = high
            rows_ref[span, (2 * part + 1) * HEAD_DIM : (2 * part + 2) * HEAD_DIM] = low

    scaling = math.log2(math.e) / math.sqrt(HEAD_DIM)
    place_row = place_row_ref[...]

    @pl.loop(0, merged_total // tile)
    def _(step):
        first = pl.multiple_of(step * tile, tile)
        merged_index = lax.broadcasted_iota(jnp.int32, (tile, row_total), 0) + first
        joins = merged_index == place_row
        counts = jnp.sum(joins.astype(jnp.float32), axis=1, keepdims=True)
        sums = jnp.dot(
            joins.astype(jnp.float32).astype(jnp.bfloat16),
            rows_ref[...],
            preferred_element_type=jnp.float32,
        )
        mean = [
            (sums[:, 2 * n * HEAD_DIM : (2 * n + 1) * HEAD_DIM]
             + sums[:, (2 * n + 1) * HEAD_DIM : (2 * n + 2) * HEAD_DIM]) / counts
            for n in range(3)
        ]
        span = pl.ds(first, tile)
        high, low = split_terms(mean[0] * scaling)
        query_cat[span, :] = jnp.concatenate([high, low], 1)
        high, low = split_terms(mean[1])
        key_high[span, :] = jnp.concatenate([high, high], 1)
        key_low[span, :] = jnp.concatenate([low, low], 1)
        high, low = split_terms(mean[2])
        value_cat[span, :] = jnp.concatenate([high, low], 1)

    contract = (((1,), (1,)), ((), ()))

    @pl.loop(0, merged_total // tile)
    def _(step):
        span = pl.ds(pl.multiple_of(step * tile, tile), tile)
        query = query_cat[span, :]
        scores = lax.dot_general(
            query, key_high[...], contract, preferred_element_type=jnp.float32
        ) + lax.dot_general(
            query, key_low[...], contract, preferred_element_type=jnp.float32
        )
        top = jnp.max(scores, axis=1, keepdims=True)
        weight = jnp.exp2(scores - top)
        total = jnp.sum(weight, axis=1, keepdims=True)
        high, low = split_terms(weight)
        mixed = jnp.dot(
            high, value_cat[...], preferred_element_type=jnp.float32
        ) + jnp.dot(low, value_cat[...], preferred_element_type=jnp.float32)
        output = (mixed[:, :HEAD_DIM] + mixed[:, HEAD_DIM:]) / total
        high, low = split_terms(output)
        output_cat[span, :] = jnp.concatenate([high, low], 1)

    for piece in range(peers):
        joined = lax.broadcasted_iota(jnp.int32, (rows, merged_total), 1) == (
            place_col_ref[piece * rows : (piece + 1) * rows, :]
        )
        both = jnp.dot(
            joined.astype(jnp.float32).astype(jnp.bfloat16),
            output_cat[...],
            preferred_element_type=jnp.float32,
        )
        returned[piece][...] = both[:, :HEAD_DIM] + both[:, HEAD_DIM:]


def attend(place_row, place_col, received):
    peers = len(received)
    rows = place_row.shape[1] // peers
    merged_total = peers * MERGED_WINDOW_ROWS
    row_total = peers * rows
    pairs = pltpu.VMEM((merged_total, 2 * HEAD_DIM), jnp.bfloat16)
    flops = 2 * merged_total * HEAD_DIM * (6 * row_total + 8 * merged_total + 2 * row_total)
    return pl.pallas_call(
        functools.partial(attend_kernel, peers),
        in_specs=[pl.BlockSpec(memory_space=pltpu.VMEM)] * (2 + peers),
        out_specs=[pl.BlockSpec(memory_space=pltpu.VMEM)] * peers,
        scratch_shapes=[pltpu.VMEM((row_total, 6 * HEAD_DIM), jnp.bfloat16)] + [pairs] * 5,
        out_shape=[jax.ShapeDtypeStruct((rows, HEAD_DIM), jnp.float32)] * peers,
        cost_estimate=pl.CostEstimate(
            flops=flops,
            transcendentals=merged_total * merged_total,
            bytes_accessed=4 * 4 * row_total * HEAD_DIM,
        ),
        name="attend",
    )(place_row, place_col, *received)


def by_heads(queries, key_rows, value_rows, merge_target):
    window_count = lax.axis_size("win")
    rows, col_width = queries.shape
    per_window = col_width // HEAD_DIM // window_count
    sources = (queries, key_rows, value_rows)
    flips = range(window_count - 1, 0, -1)

    def swap(x, flip):
        return lax.ppermute(x, "win", [(n, n ^ flip) for n in range(window_count)])

    lines = rows // HEAD_DIM
    arrived, own = [], []
    for head in range(per_window):
        got = []
        for flip in flips:
            places = merge_target.reshape(lines, HEAD_DIM) if head == 0 else None
            packed = pack(sources, flip, head, per_window, places)
            got.append(swap(packed, flip))
        arrived.append(got)
        own.append(pack(sources, 0, head, per_window))
    place = jnp.concatenate(
        [got[3 * rows : 3 * rows + lines].reshape(rows).astype(jnp.int32) for got in arrived[0]]
        + [merge_target]
    )
    place_row, place_col = place[None, :], place[:, None]
    result_shape = jax.ShapeDtypeStruct((rows, col_width), jnp.float32)
    early, late = [], []
    for head in range(per_window):
        blocks = attend(place_row, place_col, arrived[head] + [own[head]])
        early.append((0, head, blocks[-1]))
        for flip, block in zip(flips, blocks):
            (early if head < per_window - 1 else late).append((flip, head, swap(block, flip)))
    result = put_blocks(early, per_window, result_shape)
    window = lax.axis_index("win")
    for flip, head, block in (late[2], late[0], late[1]):
        result = lax.dynamic_update_slice_in_dim(
            result, block, ((window ^ flip) * per_window + head) * HEAD_DIM, 1
        )
    return result


def solution(mesh):
    spec = P(("groups", "win"), ("head", "sub"))
    window_count = mesh.shape["win"]

    def program(queries, key_rows, value_rows, merge_target):
        head_count = queries.shape[1] // HEAD_DIM // (mesh.shape["head"] * mesh.shape["sub"])
        spread = head_count % window_count == 0 and window_count & (window_count - 1) == 0

        def local(*args):
            if not spread:
                return by_windows(*args)
            return by_heads(*args)

        return jax.shard_map(
            local,
            mesh=mesh,
            in_specs=(spec, spec, spec, P(("groups", "win"))),
            out_specs=spec,
            check_vma=False,
        )(queries, key_rows, value_rows, merge_target)

    return program
```

profile of v0, /device:TPU:0, one launch (start us, length us, event | category | flops | bytes accessed | tf_op | source)
XLA Modules:
  0.0 147.2 jit_solution(7377456465241584801)
XLA Ops:
  0.0 1.8 %pack.14 = f32[776,128]{1,0:T(8,128)} custom-call(f32[256,1536]{1,0:T(8,128)} %refs_0_.23, f32[256,1536]{1,0:T(8,128)} %refs_1_.23, f32[256,1536]{1,0:T(8,128)} %refs_2_.23, s32[2,128]{1,0:T(2,128)} %bitcast.9), custom_call_target="tpu_custom_call" | custom-call | bytes 794624 | tf_op jit(solution)/shard_map/pack/pallas_call | solution.py:150
  1.8 3.1 %collective-permute-start.2 = (f32[776,128]{1,0:T(8,128)}, f32[776,128]{1,0:T(8,128)S(1)}, u32[]{:S(2)}, u32[]{:S(2)}) collective-permute-start(f32[776,128]{1,0:T(8,128)} %pack.14), channel_id=1, source_target_pairs={{0,4},{4,0},{8,12},{12,8},{1,5},{5,1},{9,13},{13,9},{2,6},{6,2},{1... | collective-permute-start | bytes 1191944 | tf_op jit(solution)/shard_map/ppermute | solution.py:306
  5.0 1.8 %pack.13 = f32[776,128]{1,0:T(8,128)} custom-call(f32[256,1536]{1,0:T(8,128)} %refs_0_.23, f32[256,1536]{1,0:T(8,128)} %refs_1_.23, f32[256,1536]{1,0:T(8,128)} %refs_2_.23, s32[2,128]{1,0:T(2,128)} %bitcast.10), custom_call_target="tpu_custom_call" | custom-call | bytes 794624 | tf_op jit(solution)/shard_map/pack/pallas_call | solution.py:150
  6.8 2.7 %collective-permute-start.1 = (f32[776,128]{1,0:T(8,128)}, f32[776,128]{1,0:T(8,128)S(1)}, u32[]{:S(2)}, u32[]{:S(2)}) collective-permute-start(f32[776,128]{1,0:T(8,128)} %pack.13), channel_id=1, source_target_pairs={{0,8},{4,12},{8,0},{12,4},{1,9},{5,13},{9,1},{13,5},{2,10},{6,14},... | collective-permute-start | bytes 1191944 | tf_op jit(solution)/shard_map/ppermute | solution.py:306
  9.5 1.8 %pack.12 = f32[776,128]{1,0:T(8,128)} custom-call(f32[256,1536]{1,0:T(8,128)} %refs_0_.23, f32[256,1536]{1,0:T(8,128)} %refs_1_.23, f32[256,1536]{1,0:T(8,128)} %refs_2_.23, s32[2,128]{1,0:T(2,128)} %bitcast.11), custom_call_target="tpu_custom_call" | custom-call | bytes 794624 | tf_op jit(solution)/shard_map/pack/pallas_call | solution.py:150
  11.3 0.1 collective-permute-start
  11.4 1.8 %pack.16 = f32[768,128]{1,0:T(8,128)} custom-call(f32[256,1536]{1,0:T(8,128)} %refs_0_.23, f32[256,1536]{1,0:T(8,128)} %refs_1_.23, f32[256,1536]{1,0:T(8,128)} %refs_2_.23), custom_call_target="tpu_custom_call" | custom-call | bytes 786432 | tf_op jit(solution)/shard_map/pack/pallas_call | solution.py:150
  13.2 3.9 %collective-permute-start.6 = (f32[768,128]{1,0:T(8,128)}, f32[768,128]{1,0:T(8,128)}, u32[]{:S(2)}, u32[]{:S(2)}) collective-permute-start(f32[768,128]{1,0:T(8,128)} %pack.16), channel_id=1, source_target_pairs={{0,12},{4,8},{8,4},{12,0},{1,13},{5,9},{9,5},{13,1},{2,14},{6,10},... | collective-permute-start | bytes 1179656 | tf_op jit(solution)/shard_map/ppermute | solution.py:306
  17.1 1.8 %pack.17 = f32[768,128]{1,0:T(8,128)} custom-call(f32[256,1536]{1,0:T(8,128)} %refs_0_.23, f32[256,1536]{1,0:T(8,128)} %refs_1_.23, f32[256,1536]{1,0:T(8,128)} %refs_2_.23), custom_call_target="tpu_custom_call" | custom-call | bytes 786432 | tf_op jit(solution)/shard_map/pack/pallas_call | solution.py:150
  18.9 0.1 collective-permute-start.7
  19.0 1.8 %pack.15.refs_3_ = f32[768,128]{1,0:T(8,128)} custom-call(f32[256,1536]{1,0:T(8,128)} %refs_0_.23, f32[256,1536]{1,0:T(8,128)} %refs_1_.23, f32[256,1536]{1,0:T(8,128)} %refs_2_.23), custom_call_target="tpu_custom_call" | custom-call | bytes 786432 | tf_op jit(solution)/shard_map/pack/pallas_call | solution.py:150
  20.8 1.8 %pack.18 = f32[768,128]{1,0:T(8,128)} custom-call(f32[256,1536]{1,0:T(8,128)} %refs_0_.23, f32[256,1536]{1,0:T(8,128)} %refs_1_.23, f32[256,1536]{1,0:T(8,128)} %refs_2_.23), custom_call_target="tpu_custom_call" | custom-call | bytes 786432 | tf_op jit(solution)/shard_map/pack/pallas_call | solution.py:150
  22.6 1.8 %pack.19.refs_3_ = f32[768,128]{1,0:T(8,128)} custom-call(f32[256,1536]{1,0:T(8,128)} %refs_0_.23, f32[256,1536]{1,0:T(8,128)} %refs_1_.23, f32[256,1536]{1,0:T(8,128)} %refs_2_.23), custom_call_target="tpu_custom_call" | custom-call | bytes 786432 | tf_op jit(solution)/shard_map/pack/pallas_call | solution.py:150
  24.5 1.8 %pack.20 = f32[768,128]{1,0:T(8,128)} custom-call(f32[256,1536]{1,0:T(8,128)} %refs_0_.23, f32[256,1536]{1,0:T(8,128)} %refs_1_.23, f32[256,1536]{1,0:T(8,128)} %refs_2_.23), custom_call_target="tpu_custom_call" | custom-call | bytes 786432 | tf_op jit(solution)/shard_map/pack/pallas_call | solution.py:150
  26.3 1.8 %pack.21 = f32[768,128]{1,0:T(8,128)} custom-call(f32[256,1536]{1,0:T(8,128)} %refs_0_.23, f32[256,1536]{1,0:T(8,128)} %refs_1_.23, f32[256,1536]{1,0:T(8,128)} %refs_2_.23), custom_call_target="tpu_custom_call" | custom-call | bytes 786432 | tf_op jit(solution)/shard_map/pack/pallas_call | solution.py:150
  28.2 1.8 %pack.22 = f32[768,128]{1,0:T(8,128)} custom-call(f32[256,1536]{1,0:T(8,128)} %refs_0_.23, f32[256,1536]{1,0:T(8,128)} %refs_1_.23, f32[256,1536]{1,0:T(8,128)} %refs_2_.23), custom_call_target="tpu_custom_call" | custom-call | bytes 786432 | tf_op jit(solution)/shard_map/pack/pallas_call | solution.py:150
  30.0 0.0 copy-start.10
  30.0 0.0 copy-start
  30.1 1.9 %pack.23.refs_3_ = f32[768,128]{1,0:T(8,128)} custom-call(f32[256,1536]{1,0:T(8,128)} %refs_0_.23, f32[256,1536]{1,0:T(8,128)} %refs_1_.23, f32[256,1536]{1,0:T(8,128)} %refs_2_.23), custom_call_target="tpu_custom_call" | custom-call | bytes 786432 | tf_op jit(solution)/shard_map/pack/pallas_call | solution.py:150
  32.0 0.0 collective-permute-done.2.refs_2_
  32.0 0.6 collective-permute-start.8
  32.7 21.3 %collective-permute-done.1.refs_1_ = f32[776,128]{1,0:T(8,128)S(1)} collective-permute-done((f32[776,128]{1,0:T(8,128)}, f32[776,128]{1,0:T(8,128)S(1)}, u32[]{:S(2)}, u32[]{:S(2)}) %collective-permute-start.1) | collective-permute-done | bytes 397344 | tf_op jit(solution)/shard_map/ppermute | solution.py:306
  54.0 2.5 %collective-permute-start.12 = (f32[768,128]{1,0:T(8,128)S(1)}, f32[768,128]{1,0:T(8,128)S(1)}, u32[]{:S(2)}, u32[]{:S(2)}) collective-permute-start(f32[768,128]{1,0:T(8,128)S(1)} %copy-done.2), channel_id=1, source_target_pairs={{0,12},{4,8},{8,4},{12,0},{1,13},{5,9},{9,5},{13,1},{2,14},{6,10},... | collective-permute-start | bytes 1179656 | tf_op jit(solution)/shard_map/ppermute | solution.py:306
  56.5 0.0 collective-permute-done.refs_0_
  56.5 16.0 %collective-permute-start.13 = (f32[768,128]{1,0:T(8,128)S(1)}, f32[768,128]{1,0:T(8,128)}, u32[]{:S(2)}, u32[]{:S(2)}) collective-permute-start(f32[768,128]{1,0:T(8,128)S(1)} %copy-done.1), channel_id=1, source_target_pairs={{0,8},{4,12},{8,0},{12,4},{1,9},{5,13},{9,1},{13,5},{2,10},{6,14},... | collective-permute-start | bytes 1179656 | tf_op jit(solution)/shard_map/ppermute | solution.py:306
  72.5 1.0 copy.5.place_col_ref
  73.6 0.0 collective-permute-done.6.refs_0_
  73.6 14.9 %collective-permute-start.14 = (f32[768,128]{1,0:T(8,128)S(1)}, f32[768,128]{1,0:T(8,128)}, u32[]{:S(2)}, u32[]{:S(2)}) collective-permute-start(f32[768,128]{1,0:T(8,128)S(1)} %copy-done), channel_id=1, source_target_pairs={{0,4},{4,0},{8,12},{12,8},{1,5},{5,1},{9,13},{13,9},{2,6},{6,2},{1... | collective-permute-start | bytes 1179656 | tf_op jit(solution)/shard_map/ppermute | solution.py:306
  88.5 0.0 copy-done.12
  88.5 0.0 copy-done.14
  88.5 10.7 %attend.3 = (f32[256,128]{1,0:T(8,128)}, f32[256,128]{1,0:T(8,128)}, f32[256,128]{1,0:T(8,128)}, f32[256,128]{1,0:T(8,128)}) custom-call(s32[1,1024]{1,0:T(1,128)} %bitcast.13, s32[1024,1]{1,0:T(8,128)} %copy.5.place_col_ref, f32[776,128]{1,0:T(8,128)} %copy-done.14, f32[776,128]{1,0:T(8,128)} %copy-done.13, f32[776,128]{1,0:T(8,128)} %copy-done.12, ...), custom_call_target="tpu_custom_call" | custom-call | flops 3162505216 | bytes 2097152 | tf_op jit(solution)/shard_map/attend/pallas_call | solution.py:283
  99.1 0.0 collective-permute-done.7.refs_1_
  99.1 2.5 %collective-permute-start.3 = (f32[256,128]{1,0:T(8,128)}, f32[256,128]{1,0:T(8,128)S(1)}, u32[]{:S(2)}, u32[]{:S(2)}) collective-permute-start(f32[256,128]{1,0:T(8,128)} %get-tuple-element.18), channel_id=1, source_target_pairs={{0,12},{4,8},{8,4},{12,0},{1,13},{5,9},{9,5},{13,1},{2,14},{6,10},... | collective-permute-start | bytes 393224 | tf_op jit(solution)/shard_map/ppermute | solution.py:306
  101.6 0.0 collective-permute-done.8.refs_2_
  101.6 0.0 collective-permute-start.4
  101.6 10.7 %attend.4 = (f32[256,128]{1,0:T(8,128)}, f32[256,128]{1,0:T(8,128)}, f32[256,128]{1,0:T(8,128)}, f32[256,128]{1,0:T(8,128)}) custom-call(s32[1,1024]{1,0:T(1,128)} %bitcast.14, s32[1024,1]{1,0:T(8,128)} %copy.5.place_col_ref, f32[768,128]{1,0:T(8,128)} %collective-permute-done.6.refs_0_, f32[768,128]{1,0:T(8,128)} %collective-permute-done.7.refs_1_, ...), custom_call_target="tpu_custom_call" | custom-call | flops 3162505216 | bytes 2097152 | tf_op jit(solution)/shard_map/attend/pallas_call | solution.py:283
  112.3 0.0 collective-permute-done.12.refs_0_
  112.3 1.9 %collective-permute-start.5 = (f32[256,128]{1,0:T(8,128)S(1)}, f32[256,128]{1,0:T(8,128)S(1)}, u32[]{:S(2)}, u32[]{:S(2)}) collective-permute-start(f32[256,128]{1,0:T(8,128)S(1)} %copy-done.16), channel_id=1, source_target_pairs={{0,4},{4,0},{8,12},{12,8},{1,5},{5,1},{9,13},{13,9},{2,6},{6,2},{1... | collective-permute-start | bytes 393224 | tf_op jit(solution)/shard_map/ppermute | solution.py:306
  114.3 4.6 %collective-permute-done.13.refs_1_ = f32[768,128]{1,0:T(8,128)} collective-permute-done((f32[768,128]{1,0:T(8,128)S(1)}, f32[768,128]{1,0:T(8,128)}, u32[]{:S(2)}, u32[]{:S(2)}) %collective-permute-start.13) | collective-permute-done | bytes 393248 | tf_op jit(solution)/shard_map/ppermute | solution.py:306
  118.9 2.5 %collective-permute-start.9 = (f32[256,128]{1,0:T(8,128)}, f32[256,128]{1,0:T(8,128)S(1)}, u32[]{:S(2)}, u32[]{:S(2)}) collective-permute-start(f32[256,128]{1,0:T(8,128)} %get-tuple-element.22), channel_id=1, source_target_pairs={{0,12},{4,8},{8,4},{12,0},{1,13},{5,9},{9,5},{13,1},{2,14},{6,10},... | collective-permute-start | bytes 393224 | tf_op jit(solution)/shard_map/ppermute | solution.py:306
  121.4 0.0 collective-permute-done.14.refs_2_
  121.4 0.0 collective-permute-start.10
  121.4 0.0 collective-permute-done.3.refs_1_
  121.4 0.0 copy-start.4
  121.4 3.6 %collective-permute-start.11 = (f32[256,128]{1,0:T(8,128)}, f32[256,128]{1,0:T(8,128)S(1)}, u32[]{:S(2)}, u32[]{:S(2)}) collective-permute-start(f32[256,128]{1,0:T(8,128)} %get-tuple-element.24), channel_id=1, source_target_pairs={{0,4},{4,0},{8,12},{12,8},{1,5},{5,1},{9,13},{13,9},{2,6},{6,2},{1... | collective-permute-start | bytes 393224 | tf_op jit(solution)/shard_map/ppermute | solution.py:306
  125.0 10.7 %attend.5 = (f32[256,128]{1,0:T(8,128)}, f32[256,128]{1,0:T(8,128)}, f32[256,128]{1,0:T(8,128)}, f32[256,128]{1,0:T(8,128)}) custom-call(s32[1,1024]{1,0:T(1,128)} %bitcast.15, s32[1024,1]{1,0:T(8,128)} %copy.5.place_col_ref, f32[768,128]{1,0:T(8,128)} %copy-done.15, f32[768,128]{1,0:T(8,128)} %collective-permute-done.13.refs_1_, ...), custom_call_target="tpu_custom_call" | custom-call | flops 3162505216 | bytes 2097152 | tf_op jit(solution)/shard_map/attend/pallas_call | solution.py:283
  135.6 0.0 copy-done.4
  135.6 0.0 collective-permute-done.4.refs_2_
  135.6 0.1 collective-permute-start.15
  135.8 0.0 collective-permute-done.5.refs_3_
  135.8 2.5 %collective-permute-start.16 = (f32[256,128]{1,0:T(8,128)}, f32[256,128]{1,0:T(8,128)S(1)}, u32[]{:S(2)}, u32[]{:S(2)}) collective-permute-start(f32[256,128]{1,0:T(8,128)} %get-tuple-element.27), channel_id=1, source_target_pairs={{0,12},{4,8},{8,4},{12,0},{1,13},{5,9},{9,5},{13,1},{2,14},{6,10},... | collective-permute-start | bytes 393224 | tf_op jit(solution)/shard_map/ppermute | solution.py:306
  138.3 0.0 collective-permute-done.9.refs_5_
  138.3 0.9 collective-permute-start.17
  139.2 0.0 collective-permute-done.10.refs_6_
  139.2 0.0 collective-permute-done.11.refs_7_
  139.2 0.6 copy-done.8
  139.8 0.1 copy-done.9
  139.9 2.4 %put_blocks.1 = f32[256,1536]{1,0:T(8,128)} custom-call(f32[256,128]{1,0:T(8,128)} %get-tuple-element.17.refs_0_, f32[256,128]{1,0:T(8,128)} %copy-done.4, f32[256,128]{1,0:T(8,128)} %copy-done.5, f32[256,128]{1,0:T(8,128)} %copy-done.6, f32[256,128]{1,0:T(8,128)} %get-tuple-element.21.refs_4_, f32[256,128]{1,0:T(8,128)} %copy-done.7, f32[256,128]{1,0:T(8,128)} %copy-done.8, ...), custom_call_target="tpu_custom_call" | custom-call | bytes 2359296 | tf_op jit(solution)/shard_map/put_blocks/pallas_call | solution.py:185
  142.3 0.7 collective-permute-done.15
  143.0 0.7 constant_dynamic-update-slice_fusion.2
  143.6 0.0 collective-permute-done.16
  143.6 0.7 constant_dynamic-update-slice_fusion.1
  144.3 2.2 %collective-permute-done.17 = f32[256,128]{1,0:T(8,128)S(1)} collective-permute-done((f32[256,128]{1,0:T(8,128)}, f32[256,128]{1,0:T(8,128)S(1)}, u32[]{:S(2)}, u32[]{:S(2)}) %collective-permute-start.17) | collective-permute-done | bytes 131104 | tf_op jit(solution)/shard_map/ppermute | solution.py:306
  146.6 0.7 constant_dynamic-update-slice_fusion
  (30 shorter events, 0.1 us)
Async XLA Ops:
  1.8 30.2 %collective-permute-start.2 = (f32[776,128]{1,0:T(8,128)}, f32[776,128]{1,0:T(8,128)S(1)}, u32[]{:S(2)}, u32[]{:S(2)}) collective-permute-start(f32[776,128]{1,0:T(8,128)} %pack.14), channel_id=1, source_target_pairs={{0,4},{4,0},{8,12},{12,8},{1,5},{5,1},{9,13},{13,9},{2,6},{6,2},{1... | collective-permute-start | bytes 1191944 | tf_op jit(solution)/shard_map/ppermute | solution.py:306
  6.8 47.2 %collective-permute-start.1 = (f32[776,128]{1,0:T(8,128)}, f32[776,128]{1,0:T(8,128)S(1)}, u32[]{:S(2)}, u32[]{:S(2)}) collective-permute-start(f32[776,128]{1,0:T(8,128)} %pack.13), channel_id=1, source_target_pairs={{0,8},{4,12},{8,0},{12,4},{1,9},{5,13},{9,1},{13,5},{2,10},{6,14},... | collective-permute-start | bytes 1191944 | tf_op jit(solution)/shard_map/ppermute | solution.py:306
  11.3 45.2 %collective-permute-start = (f32[776,128]{1,0:T(8,128)}, f32[776,128]{1,0:T(8,128)S(1)}, u32[]{:S(2)}, u32[]{:S(2)}) collective-permute-start(f32[776,128]{1,0:T(8,128)} %pack.12), channel_id=1, source_target_pairs={{0,12},{4,8},{8,4},{12,0},{1,13},{5,9},{9,5},{13,1},{2,14},{6,10},... | collective-permute-start | bytes 1191944 | tf_op jit(solution)/shard_map/ppermute | solution.py:306
  13.2 60.4 %collective-permute-start.6 = (f32[768,128]{1,0:T(8,128)}, f32[768,128]{1,0:T(8,128)}, u32[]{:S(2)}, u32[]{:S(2)}) collective-permute-start(f32[768,128]{1,0:T(8,128)} %pack.16), channel_id=1, source_target_pairs={{0,12},{4,8},{8,4},{12,0},{1,13},{5,9},{9,5},{13,1},{2,14},{6,10},... | collective-permute-start | bytes 1179656 | tf_op jit(solution)/shard_map/ppermute | solution.py:306
  18.9 80.2 %collective-permute-start.7 = (f32[768,128]{1,0:T(8,128)}, f32[768,128]{1,0:T(8,128)}, u32[]{:S(2)}, u32[]{:S(2)}) collective-permute-start(f32[768,128]{1,0:T(8,128)} %pack.17), channel_id=1, source_target_pairs={{0,8},{4,12},{8,0},{12,4},{1,9},{5,13},{9,1},{13,5},{2,10},{6,14},... | collective-permute-start | bytes 1179656 | tf_op jit(solution)/shard_map/ppermute | solution.py:306
  30.0 2.0 %copy-start.3 = (f32[768,128]{1,0:T(8,128)S(1)}, f32[768,128]{1,0:T(8,128)}, u32[]{:S(2)}) copy-start(f32[768,128]{1,0:T(8,128)} %pack.18) | copy-start | bytes 1179652
  30.0 24.0 %copy-start.2 = (f32[768,128]{1,0:T(8,128)S(1)}, f32[768,128]{1,0:T(8,128)}, u32[]{:S(2)}) copy-start(f32[768,128]{1,0:T(8,128)} %pack.20) | copy-start | bytes 1179652
  30.0 26.5 %copy-start.1 = (f32[768,128]{1,0:T(8,128)S(1)}, f32[768,128]{1,0:T(8,128)}, u32[]{:S(2)}) copy-start(f32[768,128]{1,0:T(8,128)} %pack.21) | copy-start | bytes 1179652
  30.0 42.5 %copy-start.10 = (s32[256]{0:T(256)S(1)}, s32[256]{0:T(256)}, u32[]{:S(2)}) copy-start(s32[256]{0:T(256)} %param.7) | copy-start | bytes 3076
  30.0 43.5 %copy-start = (f32[768,128]{1,0:T(8,128)S(1)}, f32[768,128]{1,0:T(8,128)}, u32[]{:S(2)}) copy-start(f32[768,128]{1,0:T(8,128)} %pack.22) | copy-start | bytes 1179652
  32.0 56.4 %copy-start.12 = (f32[776,128]{1,0:T(8,128)}, f32[776,128]{1,0:T(8,128)S(1)}, u32[]{:S(2)}) copy-start(f32[776,128]{1,0:T(8,128)S(1)} %collective-permute-done.2.refs_2_) | copy-start | bytes 1191940
  32.0 69.6 %collective-permute-start.8 = (f32[768,128]{1,0:T(8,128)S(1)}, f32[768,128]{1,0:T(8,128)}, u32[]{:S(2)}, u32[]{:S(2)}) collective-permute-start(f32[768,128]{1,0:T(8,128)S(1)} %copy-done.3), channel_id=1, source_target_pairs={{0,4},{4,0},{8,12},{12,8},{1,5},{5,1},{9,13},{13,9},{2,6},{6,2},{1... | collective-permute-start | bytes 1179656 | tf_op jit(solution)/shard_map/ppermute | solution.py:306
  54.0 34.5 %copy-start.13 = (f32[776,128]{1,0:T(8,128)}, f32[776,128]{1,0:T(8,128)S(1)}, u32[]{:S(2)}) copy-start(f32[776,128]{1,0:T(8,128)S(1)} %collective-permute-done.1.refs_1_) | copy-start | bytes 1191940
  54.0 58.3 %collective-permute-start.12 = (f32[768,128]{1,0:T(8,128)S(1)}, f32[768,128]{1,0:T(8,128)S(1)}, u32[]{:S(2)}, u32[]{:S(2)}) collective-permute-start(f32[768,128]{1,0:T(8,128)S(1)} %copy-done.2), channel_id=1, source_target_pairs={{0,12},{4,8},{8,4},{12,0},{1,13},{5,9},{9,5},{13,1},{2,14},{6,10},... | collective-permute-start | bytes 1179656 | tf_op jit(solution)/shard_map/ppermute | solution.py:306
  56.5 32.0 %copy-start.14 = (f32[776,128]{1,0:T(8,128)}, f32[776,128]{1,0:T(8,128)S(1)}, u32[]{:S(2)}) copy-start(f32[776,128]{1,0:T(8,128)S(1)} %collective-permute-done.refs_0_) | copy-start | bytes 1191940
  56.5 62.4 %collective-permute-start.13 = (f32[768,128]{1,0:T(8,128)S(1)}, f32[768,128]{1,0:T(8,128)}, u32[]{:S(2)}, u32[]{:S(2)}) collective-permute-start(f32[768,128]{1,0:T(8,128)S(1)} %copy-done.1), channel_id=1, source_target_pairs={{0,8},{4,12},{8,0},{12,4},{1,9},{5,13},{9,1},{13,5},{2,10},{6,14},... | collective-permute-start | bytes 1179656 | tf_op jit(solution)/shard_map/ppermute | solution.py:306
  72.5 15.9 %copy-start.11 = (s32[1024]{0:T(1024)}, s32[1024]{0:T(1024)S(1)}, u32[]{:S(2)}) copy-start(s32[1024]{0:T(1024)S(1)} %pad_add_fusion) | copy-start | bytes 12292
  73.6 47.8 %collective-permute-start.14 = (f32[768,128]{1,0:T(8,128)S(1)}, f32[768,128]{1,0:T(8,128)}, u32[]{:S(2)}, u32[]{:S(2)}) collective-permute-start(f32[768,128]{1,0:T(8,128)S(1)} %copy-done), channel_id=1, source_target_pairs={{0,4},{4,0},{8,12},{12,8},{1,5},{5,1},{9,13},{13,9},{2,6},{6,2},{1... | collective-permute-start | bytes 1179656 | tf_op jit(solution)/shard_map/ppermute | solution.py:306
  99.1 22.2 %collective-permute-start.3 = (f32[256,128]{1,0:T(8,128)}, f32[256,128]{1,0:T(8,128)S(1)}, u32[]{:S(2)}, u32[]{:S(2)}) collective-permute-start(f32[256,128]{1,0:T(8,128)} %get-tuple-element.18), channel_id=1, source_target_pairs={{0,12},{4,8},{8,4},{12,0},{1,13},{5,9},{9,5},{13,1},{2,14},{6,10},... | collective-permute-start | bytes 393224 | tf_op jit(solution)/shard_map/ppermute | solution.py:306
  101.6 10.7 %copy-start.16 = (f32[256,128]{1,0:T(8,128)S(1)}, f32[256,128]{1,0:T(8,128)}, u32[]{:S(2)}) copy-start(f32[256,128]{1,0:T(8,128)} %get-tuple-element.20) | copy-start | bytes 393220
  101.6 34.0 %collective-permute-start.4 = (f32[256,128]{1,0:T(8,128)}, f32[256,128]{1,0:T(8,128)S(1)}, u32[]{:S(2)}, u32[]{:S(2)}) collective-permute-start(f32[256,128]{1,0:T(8,128)} %get-tuple-element.19), channel_id=1, source_target_pairs={{0,8},{4,12},{8,0},{12,4},{1,9},{5,13},{9,1},{13,5},{2,10},{6,14},... | collective-permute-start | bytes 393224 | tf_op jit(solution)/shard_map/ppermute | solution.py:306
  112.3 12.6 %copy-start.15 = (f32[768,128]{1,0:T(8,128)}, f32[768,128]{1,0:T(8,128)S(1)}, u32[]{:S(2)}) copy-start(f32[768,128]{1,0:T(8,128)S(1)} %collective-permute-done.12.refs_0_) | copy-start | bytes 1179652
  112.3 23.4 %collective-permute-start.5 = (f32[256,128]{1,0:T(8,128)S(1)}, f32[256,128]{1,0:T(8,128)S(1)}, u32[]{:S(2)}, u32[]{:S(2)}) collective-permute-start(f32[256,128]{1,0:T(8,128)S(1)} %copy-done.16), channel_id=1, source_target_pairs={{0,4},{4,0},{8,12},{12,8},{1,5},{5,1},{9,13},{13,9},{2,6},{6,2},{1... | collective-permute-start | bytes 393224 | tf_op jit(solution)/shard_map/ppermute | solution.py:306
  118.9 19.4 %collective-permute-start.9 = (f32[256,128]{1,0:T(8,128)}, f32[256,128]{1,0:T(8,128)S(1)}, u32[]{:S(2)}, u32[]{:S(2)}) collective-permute-start(f32[256,128]{1,0:T(8,128)} %get-tuple-element.22), channel_id=1, source_target_pairs={{0,12},{4,8},{8,4},{12,0},{1,13},{5,9},{9,5},{13,1},{2,14},{6,10},... | collective-permute-start | bytes 393224 | tf_op jit(solution)/shard_map/ppermute | solution.py:306
  121.4 17.8 %collective-permute-start.10 = (f32[256,128]{1,0:T(8,128)}, f32[256,128]{1,0:T(8,128)S(1)}, u32[]{:S(2)}, u32[]{:S(2)}) collective-permute-start(f32[256,128]{1,0:T(8,128)} %get-tuple-element.23), channel_id=1, source_target_pairs={{0,8},{4,12},{8,0},{12,4},{1,9},{5,13},{9,1},{13,5},{2,10},{6,14},... | collective-permute-start | bytes 393224 | tf_op jit(solution)/shard_map/ppermute | solution.py:306
  121.4 14.2 %copy-start.4 = (f32[256,128]{1,0:T(8,128)}, f32[256,128]{1,0:T(8,128)S(1)}, u32[]{:S(2)}) copy-start(f32[256,128]{1,0:T(8,128)S(1)} %collective-permute-done.3.refs_1_) | copy-start | bytes 393220
  121.4 17.8 %collective-permute-start.11 = (f32[256,128]{1,0:T(8,128)}, f32[256,128]{1,0:T(8,128)S(1)}, u32[]{:S(2)}, u32[]{:S(2)}) collective-permute-start(f32[256,128]{1,0:T(8,128)} %get-tuple-element.24), channel_id=1, source_target_pairs={{0,4},{4,0},{8,12},{12,8},{1,5},{5,1},{9,13},{13,9},{2,6},{6,2},{1... | collective-permute-start | bytes 393224 | tf_op jit(solution)/shard_map/ppermute | solution.py:306
  135.6 3.6 %copy-start.5 = (f32[256,128]{1,0:T(8,128)}, f32[256,128]{1,0:T(8,128)S(1)}, u32[]{:S(2)}) copy-start(f32[256,128]{1,0:T(8,128)S(1)} %collective-permute-done.4.refs_2_) | copy-start | bytes 393220
  135.6 7.3 %collective-permute-start.15 = (f32[256,128]{1,0:T(8,128)}, f32[256,128]{1,0:T(8,128)S(1)}, u32[]{:S(2)}, u32[]{:S(2)}) collective-permute-start(f32[256,128]{1,0:T(8,128)} %get-tuple-element.26), channel_id=1, source_target_pairs={{0,4},{4,0},{8,12},{12,8},{1,5},{5,1},{9,13},{13,9},{2,6},{6,2},{1... | collective-permute-start | bytes 393224 | tf_op jit(solution)/shard_map/ppermute | solution.py:306
  135.8 3.5 %copy-start.6 = (f32[256,128]{1,0:T(8,128)}, f32[256,128]{1,0:T(8,128)S(1)}, u32[]{:S(2)}) copy-start(f32[256,128]{1,0:T(8,128)S(1)} %collective-permute-done.5.refs_3_) | copy-start | bytes 393220
  135.8 7.9 %collective-permute-start.16 = (f32[256,128]{1,0:T(8,128)}, f32[256,128]{1,0:T(8,128)S(1)}, u32[]{:S(2)}, u32[]{:S(2)}) collective-permute-start(f32[256,128]{1,0:T(8,128)} %get-tuple-element.27), channel_id=1, source_target_pairs={{0,12},{4,8},{8,4},{12,0},{1,13},{5,9},{9,5},{13,1},{2,14},{6,10},... | collective-permute-start | bytes 393224 | tf_op jit(solution)/shard_map/ppermute | solution.py:306
  138.3 1.0 copy-start.7
  138.3 8.3 %collective-permute-start.17 = (f32[256,128]{1,0:T(8,128)}, f32[256,128]{1,0:T(8,128)S(1)}, u32[]{:S(2)}, u32[]{:S(2)}) collective-permute-start(f32[256,128]{1,0:T(8,128)} %get-tuple-element.28), channel_id=1, source_target_pairs={{0,8},{4,12},{8,0},{12,4},{1,9},{5,13},{9,1},{13,5},{2,10},{6,14},... | collective-permute-start | bytes 393224 | tf_op jit(solution)/shard_map/ppermute | solution.py:306
  139.2 0.6 copy-start.8
  139.2 0.7 copy-start.9
where the time goes:
time: 148 us; the launch traced here: 147 us
  starting transfers between devices  57.8 us (39%)
  Pallas kernels  56.5 us (38%)
  waiting for transfers between devices  28.9 us (20%)
  local copies, waits for them, and re-layouts  3.75 us (3%)
    ppermute x18, starting transfers between devices, swap(): return lax.ppermute(x, 'win', [(n, n ^ flip) for n in range(window_count)])  57.8 us
    pallas_call x3, Pallas kernels, attend(): pl.pallas_call(functools.partial(attend_kernel, peers), in_specs=[pl.Bloc...  32 us
    ppermute x18, waiting for transfers between devices, swap(): return lax.ppermute(x, 'win', [(n, n ^ flip) for n in range(window_count)])  28.9 us
    pallas_call x12, Pallas kernels, pack(): pl.pallas_call(functools.partial(pack_kernel, flip, head, per_window, tai...  22 us
  transfers between devices with their start and end apart: 18, of which 4 were waited for; matrix products, arithmetic and copies ran while one was open for 2% of the time, Pallas kernels for 37%

commit v1 on v0

--- a/solution.py
+++ b/solution.py
@@ -109,10 +109,15 @@
     return returned.reshape(-1, col_width)[slot_index]
 
 
-def split_terms(x):
-    high = x.astype(jnp.bfloat16)
-    low = (x - high.astype(jnp.float32)).astype(jnp.bfloat16)
-    return high, low
+def split_terms(x, count):
+    terms = []
+    for _ in range(count):
+        terms.append(x.astype(jnp.bfloat16))
+        x = x - terms[-1].astype(jnp.float32)
+    return terms
+
+
+TERMS = (3, 3, 2)
 
 
 def pack_kernel(flip, head, per_window, tailed, *refs):
@@ -198,68 +203,72 @@
 
 def attend_kernel(peers, place_row_ref, place_col_ref, *refs):
     received, returned = refs[:peers], refs[peers : 2 * peers]
-    rows_ref, query_cat, key_high, key_low, value_cat, output_cat = refs[2 * peers :]
+    rows_ref, query_main, query_rest, key_high, key_mid, key_rest, value_cat, output_cat = refs[
+        2 * peers :
+    ]
     rows = returned[0].shape[0]
     row_total = rows * peers
-    merged_total = query_cat.shape[0]
+    merged_total = query_main.shape[0]
     tile = MERGED_WINDOW_ROWS
 
-    for part in range(3):
-        for piece in range(peers):
-            high, low = split_terms(received[piece][part * rows : (part + 1) * rows, :])
-            span = slice(piece * rows, (piece + 1) * rows)
-            rows_ref[span, 2 * part * HEAD_DIM : (2 * part + 1) * HEAD_DIM] = high
-            rows_ref[span, (2 * part + 1) * HEAD_DIM : (2 * part + 2) * HEAD_DIM] = low
+    for piece in range(peers):
+        column = 0
+        for part, count in enumerate(TERMS):
+            block = received[piece][part * rows : (part + 1) * rows, :]
+            for term in split_terms(block, count):
+                rows_ref[piece * rows : (piece + 1) * rows, column : column + HEAD_DIM] = term
+                column += HEAD_DIM
 
     scaling = math.log2(math.e) / math.sqrt(HEAD_DIM)
     place_row = place_row_ref[...]
 
-    @pl.loop(0, merged_total // tile)
-    def _(step):
-        first = pl.multiple_of(step * tile, tile)
+    for first in range(0, merged_total, tile):
         merged_index = lax.broadcasted_iota(jnp.int32, (tile, row_total), 0) + first
-        joins = merged_index == place_row
-        counts = jnp.sum(joins.astype(jnp.float32), axis=1, keepdims=True)
+        joins = (merged_index == place_row).astype(jnp.float32)
+        counts = jnp.sum(joins, axis=1, keepdims=True)
         sums = jnp.dot(
-            joins.astype(jnp.float32).astype(jnp.bfloat16),
-            rows_ref[...],
-            preferred_element_type=jnp.float32,
-        )
-        mean = [
-            (sums[:, 2 * n * HEAD_DIM : (2 * n + 1) * HEAD_DIM]
-             + sums[:, (2 * n + 1) * HEAD_DIM : (2 * n + 2) * HEAD_DIM]) / counts
-            for n in range(3)
-        ]
-        span = pl.ds(first, tile)
-        high, low = split_terms(mean[0] * scaling)
-        query_cat[span, :] = jnp.concatenate([high, low], 1)
-        high, low = split_terms(mean[1])
+            joins.astype(jnp.bfloat16), rows_ref[...], preferred_element_type=jnp.float32
+        )
+        means = []
+        column = 0
+        for count in TERMS:
+            terms = [
+                sums[:, column + n * HEAD_DIM : column + (n + 1) * HEAD_DIM] for n in range(count)
+            ]
+            means.append(sum(terms[-2::-1], terms[-1]) / counts)
+            column += count * HEAD_DIM
+        span = slice(first, first + tile)
+        high, mid, low = split_terms(means[0] * scaling, 3)
+        query_main[span, :] = jnp.concatenate([high, mid], 1)
+        query_rest[span, :] = jnp.concatenate([high, low], 1)
+        high, mid, low = split_terms(means[1], 3)
         key_high[span, :] = jnp.concatenate([high, high], 1)
-        key_low[span, :] = jnp.concatenate([low, low], 1)
-        high, low = split_terms(mean[2])
-        value_cat[span, :] = jnp.concatenate([high, low], 1)
+        key_mid[span, :] = jnp.concatenate([mid, mid], 1)
+        key_rest[span, :] = jnp.concatenate([low, high], 1)
+        value_cat[span, :] = jnp.concatenate(split_terms(means[2], 2), 1)
 
     contract = (((1,), (1,)), ((), ()))
 
-    @pl.loop(0, merged_total // tile)
-    def _(step):
-        span = pl.ds(pl.multiple_of(step * tile, tile), tile)
-        query = query_cat[span, :]
-        scores = lax.dot_general(
-            query, key_high[...], contract, preferred_element_type=jnp.float32
-        ) + lax.dot_general(
-            query, key_low[...], contract, preferred_element_type=jnp.float32
-        )
+    for first in range(0, merged_total, tile):
+        span = slice(first, first + tile)
+        scores = 0.0
+        for query, key in (
+            (query_rest, key_rest),
+            (query_main, key_mid),
+            (query_main, key_high),
+        ):
+            scores += lax.dot_general(
+                query[span, :], key[...], contract, preferred_element_type=jnp.float32
+            )
         top = jnp.max(scores, axis=1, keepdims=True)
         weight = jnp.exp2(scores - top)
         total = jnp.sum(weight, axis=1, keepdims=True)
-        high, low = split_terms(weight)
+        high, low = split_terms(weight, 2)
         mixed = jnp.dot(
             high, value_cat[...], preferred_element_type=jnp.float32
         ) + jnp.dot(low, value_cat[...], preferred_element_type=jnp.float32)
         output = (mixed[:, :HEAD_DIM] + mixed[:, HEAD_DIM:]) / total
-        high, low = split_terms(output)
-        output_cat[span, :] = jnp.concatenate([high, low], 1)
+        output_cat[span, :] = jnp.concatenate(split_terms(output, 2), 1)
 
     for piece in range(peers):
         joined = lax.broadcasted_iota(jnp.int32, (rows, merged_total), 1) == (
@@ -279,12 +288,12 @@
     merged_total = peers * MERGED_WINDOW_ROWS
     row_total = peers * rows
     pairs = pltpu.VMEM((merged_total, 2 * HEAD_DIM), jnp.bfloat16)
-    flops = 2 * merged_total * HEAD_DIM * (6 * row_total + 8 * merged_total + 2 * row_total)
+    flops = 2 * merged_total * HEAD_DIM * (10 * row_total + 10 * merged_total)
     return pl.pallas_call(
         functools.partial(attend_kernel, peers),
         in_specs=[pl.BlockSpec(memory_space=pltpu.VMEM)] * (2 + peers),
         out_specs=[pl.BlockSpec(memory_space=pltpu.VMEM)] * peers,
-        scratch_shapes=[pltpu.VMEM((row_total, 6 * HEAD_DIM), jnp.bfloat16)] + [pairs] * 5,
+        scratch_shapes=[pltpu.VMEM((row_total, sum(TERMS) * HEAD_DIM), jnp.bfloat16)] + [pairs] * 7,
         out_shape=[jax.ShapeDtypeStruct((rows, HEAD_DIM), jnp.float32)] * peers,
         cost_estimate=pl.CostEstimate(
             flops=flops,
@@ -326,10 +335,10 @@
         blocks = attend(place_row, place_col, arrived[head] + [own[head]])
         early.append((0, head, blocks[-1]))
         for flip, block in zip(flips, blocks):
-            (early if head < per_window - 1 else late).append((flip, head, swap(block, flip)))
+            (early if head == 0 else late).append((flip, head, swap(block, flip)))
     result = put_blocks(early, per_window, result_shape)
     window = lax.axis_index("win")
-    for flip, head, block in (late[2], late[0], late[1]):
+    for flip, head, block in (*late[2:3], *late[1::-1], late[5], *late[3:5]):
         result = lax.dynamic_update_slice_in_dim(
             result, block, ((window ^ flip) * per_window + head) * HEAD_DIM, 1
         )

time: 148 us -> 147 us (level)
  waiting for transfers between devices: 28.9 us -> 39.3 us
  starting transfers between devices: 57.8 us -> 51.4 us
  Pallas kernels: 56.5 us -> 50.5 us
    ppermute x18, waiting for transfers between devices: 28.9 us -> 39.3 us  [swap(): return lax.ppermute(x, 'win', [(n, n ^ flip) for n in range(window_count)])]
    ppermute x18, starting transfers between devices: 57.8 us -> 51.4 us  [swap(): return lax.ppermute(x, 'win', [(n, n ^ flip) for n in range(window_count)])]
    pallas_call x3, Pallas kernels: 32 us -> 26.3 us  [attend(): pl.pallas_call(functools.partial(attend_kernel, peers), in_specs=[pl.Bloc...]
    dynamic_update_slice x3 -> x6, local copies, waits for them, and re-layouts: 1.99 us -> 3.98 us  [by_heads(): lax.dynamic_update_slice_in_dim(result, block, ((window ^ flip) * per_win...]
  transfers between devices with their start and end apart: 18 -> 18, of which waited for: 4 -> 4; matrix products, arithmetic and copies ran while one was open for 2% -> 3% of each run, Pallas kernels for 37% -> 33%
where the time goes in v1:
time: 147 us
  starting transfers between devices  51.4 us (35%)
  Pallas kernels  50.5 us (34%)
  waiting for transfers between devices  39.3 us (27%)
  local copies, waits for them, and re-layouts  5.08 us (3%)
    ppermute x18, starting transfers between devices, swap(): return lax.ppermute(x, 'win', [(n, n ^ flip) for n in range(window_count)])  51.4 us
    ppermute x18, waiting for transfers between devices, swap(): return lax.ppermute(x, 'win', [(n, n ^ flip) for n in range(window_count)])  39.3 us
    pallas_call x3, Pallas kernels, attend(): pl.pallas_call(functools.partial(attend_kernel, peers), in_specs=[pl.Bloc...  26.3 us
    pallas_call x12, Pallas kernels, pack(): pl.pallas_call(functools.partial(pack_kernel, flip, head, per_window, tai...  22 us
    dynamic_update_slice x6, local copies, waits for them, and re-layouts, by_heads(): lax.dynamic_update_slice_in_dim(result, block, ((window ^ flip) * per_win...  3.98 us
  transfers between devices with their start and end apart: 18, of which 4 were waited for; matrix products, arithmetic and copies ran while one was open for 3% of the time, Pallas kernels for 33%

profile of v1, /device:TPU:0, one launch (start us, length us, event | category | flops | bytes accessed | tf_op | source)
XLA Modules:
  0.0 146.7 jit_solution(4837950870132933589)
XLA Ops:
  0.0 1.8 %pack.14 = f32[776,128]{1,0:T(8,128)} custom-call(f32[256,1536]{1,0:T(8,128)} %refs_0_.23, f32[256,1536]{1,0:T(8,128)} %refs_1_.23, f32[256,1536]{1,0:T(8,128)} %refs_2_.23, s32[2,128]{1,0:T(2,128)} %bitcast.9), custom_call_target="tpu_custom_call" | custom-call | bytes 794624 | tf_op jit(solution)/shard_map/pack/pallas_call | solution.py:155
  1.8 3.1 %collective-permute-start.2 = (f32[776,128]{1,0:T(8,128)}, f32[776,128]{1,0:T(8,128)S(1)}, u32[]{:S(2)}, u32[]{:S(2)}) collective-permute-start(f32[776,128]{1,0:T(8,128)} %pack.14), channel_id=1, source_target_pairs={{0,4},{4,0},{8,12},{12,8},{1,5},{5,1},{9,13},{13,9},{2,6},{6,2},{1... | collective-permute-start | bytes 1191944 | tf_op jit(solution)/shard_map/ppermute | solution.py:315
  5.0 1.8 %pack.13 = f32[776,128]{1,0:T(8,128)} custom-call(f32[256,1536]{1,0:T(8,128)} %refs_0_.23, f32[256,1536]{1,0:T(8,128)} %refs_1_.23, f32[256,1536]{1,0:T(8,128)} %refs_2_.23, s32[2,128]{1,0:T(2,128)} %bitcast.10), custom_call_target="tpu_custom_call" | custom-call | bytes 794624 | tf_op jit(solution)/shard_map/pack/pallas_call | solution.py:155
  6.8 2.7 %collective-permute-start.1 = (f32[776,128]{1,0:T(8,128)}, f32[776,128]{1,0:T(8,128)S(1)}, u32[]{:S(2)}, u32[]{:S(2)}) collective-permute-start(f32[776,128]{1,0:T(8,128)} %pack.13), channel_id=1, source_target_pairs={{0,8},{4,12},{8,0},{12,4},{1,9},{5,13},{9,1},{13,5},{2,10},{6,14},... | collective-permute-start | bytes 1191944 | tf_op jit(solution)/shard_map/ppermute | solution.py:315
  9.5 1.8 %pack.12 = f32[776,128]{1,0:T(8,128)} custom-call(f32[256,1536]{1,0:T(8,128)} %refs_0_.23, f32[256,1536]{1,0:T(8,128)} %refs_1_.23, f32[256,1536]{1,0:T(8,128)} %refs_2_.23, s32[2,128]{1,0:T(2,128)} %bitcast.11), custom_call_target="tpu_custom_call" | custom-call | bytes 794624 | tf_op jit(solution)/shard_map/pack/pallas_call | solution.py:155
  11.3 0.1 collective-permute-start
  11.4 1.8 %pack.21 = f32[768,128]{1,0:T(8,128)} custom-call(f32[256,1536]{1,0:T(8,128)} %refs_0_.23, f32[256,1536]{1,0:T(8,128)} %refs_1_.23, f32[256,1536]{1,0:T(8,128)} %refs_2_.23), custom_call_target="tpu_custom_call" | custom-call | bytes 786432 | tf_op jit(solution)/shard_map/pack/pallas_call | solution.py:155
  13.2 1.9 %collective-permute-start.10 = (f32[768,128]{1,0:T(8,128)}, f32[768,128]{1,0:T(8,128)S(1)}, u32[]{:S(2)}, u32[]{:S(2)}) collective-permute-start(f32[768,128]{1,0:T(8,128)} %pack.21), channel_id=1, source_target_pairs={{0,8},{4,12},{8,0},{12,4},{1,9},{5,13},{9,1},{13,5},{2,10},{6,14},... | collective-permute-start | bytes 1179656 | tf_op jit(solution)/shard_map/ppermute | solution.py:315
  15.2 1.8 %pack.22 = f32[768,128]{1,0:T(8,128)} custom-call(f32[256,1536]{1,0:T(8,128)} %refs_0_.23, f32[256,1536]{1,0:T(8,128)} %refs_1_.23, f32[256,1536]{1,0:T(8,128)} %refs_2_.23), custom_call_target="tpu_custom_call" | custom-call | bytes 786432 | tf_op jit(solution)/shard_map/pack/pallas_call | solution.py:155
  17.0 2.5 %collective-permute-start.11 = (f32[768,128]{1,0:T(8,128)}, f32[768,128]{1,0:T(8,128)}, u32[]{:S(2)}, u32[]{:S(2)}) collective-permute-start(f32[768,128]{1,0:T(8,128)} %pack.22), channel_id=1, source_target_pairs={{0,4},{4,0},{8,12},{12,8},{1,5},{5,1},{9,13},{13,9},{2,6},{6,2},{1... | collective-permute-start | bytes 1179656 | tf_op jit(solution)/shard_map/ppermute | solution.py:315
  19.5 1.8 %pack.15.refs_3_ = f32[768,128]{1,0:T(8,128)} custom-call(f32[256,1536]{1,0:T(8,128)} %refs_0_.23, f32[256,1536]{1,0:T(8,128)} %refs_1_.23, f32[256,1536]{1,0:T(8,128)} %refs_2_.23), custom_call_target="tpu_custom_call" | custom-call | bytes 786432 | tf_op jit(solution)/shard_map/pack/pallas_call | solution.py:155
  21.4 1.8 %pack.20 = f32[768,128]{1,0:T(8,128)} custom-call(f32[256,1536]{1,0:T(8,128)} %refs_0_.23, f32[256,1536]{1,0:T(8,128)} %refs_1_.23, f32[256,1536]{1,0:T(8,128)} %refs_2_.23), custom_call_target="tpu_custom_call" | custom-call | bytes 786432 | tf_op jit(solution)/shard_map/pack/pallas_call | solution.py:155
  23.2 1.8 %pack.23.refs_3_ = f32[768,128]{1,0:T(8,128)} custom-call(f32[256,1536]{1,0:T(8,128)} %refs_0_.23, f32[256,1536]{1,0:T(8,128)} %refs_1_.23, f32[256,1536]{1,0:T(8,128)} %refs_2_.23), custom_call_target="tpu_custom_call" | custom-call | bytes 786432 | tf_op jit(solution)/shard_map/pack/pallas_call | solution.py:155
  25.1 1.8 %pack.16 = f32[768,128]{1,0:T(8,128)} custom-call(f32[256,1536]{1,0:T(8,128)} %refs_0_.23, f32[256,1536]{1,0:T(8,128)} %refs_1_.23, f32[256,1536]{1,0:T(8,128)} %refs_2_.23), custom_call_target="tpu_custom_call" | custom-call | bytes 786432 | tf_op jit(solution)/shard_map/pack/pallas_call | solution.py:155
  26.9 1.8 %pack.17 = f32[768,128]{1,0:T(8,128)} custom-call(f32[256,1536]{1,0:T(8,128)} %refs_0_.23, f32[256,1536]{1,0:T(8,128)} %refs_1_.23, f32[256,1536]{1,0:T(8,128)} %refs_2_.23), custom_call_target="tpu_custom_call" | custom-call | bytes 786432 | tf_op jit(solution)/shard_map/pack/pallas_call | solution.py:155
  28.7 1.8 %pack.18 = f32[768,128]{1,0:T(8,128)} custom-call(f32[256,1536]{1,0:T(8,128)} %refs_0_.23, f32[256,1536]{1,0:T(8,128)} %refs_1_.23, f32[256,1536]{1,0:T(8,128)} %refs_2_.23), custom_call_target="tpu_custom_call" | custom-call | bytes 786432 | tf_op jit(solution)/shard_map/pack/pallas_call | solution.py:155
  30.5 0.0 copy-start.3
  30.5 0.0 copy-start.2
  30.6 0.0 copy-start.1
  30.6 0.0 copy-start.7
  30.6 1.9 %pack.19.refs_3_ = f32[768,128]{1,0:T(8,128)} custom-call(f32[256,1536]{1,0:T(8,128)} %refs_0_.23, f32[256,1536]{1,0:T(8,128)} %refs_1_.23, f32[256,1536]{1,0:T(8,128)} %refs_2_.23), custom_call_target="tpu_custom_call" | custom-call | bytes 786432 | tf_op jit(solution)/shard_map/pack/pallas_call | solution.py:155
  32.6 0.0 collective-permute-done.2.refs_2_
  32.6 0.1 collective-permute-start.6
  32.7 12.9 %collective-permute-done.1.refs_1_ = f32[776,128]{1,0:T(8,128)S(1)} collective-permute-done((f32[776,128]{1,0:T(8,128)}, f32[776,128]{1,0:T(8,128)S(1)}, u32[]{:S(2)}, u32[]{:S(2)}) %collective-permute-start.1) | collective-permute-done | bytes 397344 | tf_op jit(solution)/shard_map/ppermute | solution.py:315
  45.6 0.0 collective-permute-start.7
  45.6 0.0 collective-permute-done.refs_0_
  45.6 25.9 %collective-permute-start.8 = (f32[768,128]{1,0:T(8,128)S(1)}, f32[768,128]{1,0:T(8,128)}, u32[]{:S(2)}, u32[]{:S(2)}) collective-permute-start(f32[768,128]{1,0:T(8,128)S(1)} %copy-done.1), channel_id=1, source_target_pairs={{0,4},{4,0},{8,12},{12,8},{1,5},{5,1},{9,13},{13,9},{2,6},{6,2},{1... | collective-permute-start | bytes 1179656 | tf_op jit(solution)/shard_map/ppermute | solution.py:315
  71.5 1.0 copy.5.place_col_ref
  72.6 0.0 collective-permute-done.6.refs_0_
  72.6 2.5 %collective-permute-start.9 = (f32[768,128]{1,0:T(8,128)S(1)}, f32[768,128]{1,0:T(8,128)S(1)}, u32[]{:S(2)}, u32[]{:S(2)}) collective-permute-start(f32[768,128]{1,0:T(8,128)S(1)} %copy-done), channel_id=1, source_target_pairs={{0,12},{4,8},{8,4},{12,0},{1,13},{5,9},{9,5},{13,1},{2,14},{6,10},... | collective-permute-start | bytes 1179656 | tf_op jit(solution)/shard_map/ppermute | solution.py:315
  75.0 0.0 copy-done.9
  75.1 8.8 %attend.3 = (f32[256,128]{1,0:T(8,128)}, f32[256,128]{1,0:T(8,128)}, f32[256,128]{1,0:T(8,128)}, f32[256,128]{1,0:T(8,128)}) custom-call(s32[1,1024]{1,0:T(1,128)} %bitcast.13, s32[1024,1]{1,0:T(8,128)} %copy.5.place_col_ref, f32[776,128]{1,0:T(8,128)} %copy-done.11, f32[776,128]{1,0:T(8,128)} %copy-done.10, f32[776,128]{1,0:T(8,128)} %copy-done.9, ...), custom_call_target="tpu_custom_call" | custom-call | flops 3953131520 | bytes 2097152 | tf_op jit(solution)/shard_map/attend/pallas_call | solution.py:292
  83.8 21.0 %collective-permute-done.7.refs_1_ = f32[768,128]{1,0:T(8,128)} collective-permute-done((f32[768,128]{1,0:T(8,128)S(1)}, f32[768,128]{1,0:T(8,128)}, u32[]{:S(2)}, u32[]{:S(2)}) %collective-permute-start.7) | collective-permute-done | bytes 393248 | tf_op jit(solution)/shard_map/ppermute | solution.py:315
  104.8 2.5 %collective-permute-start.3 = (f32[256,128]{1,0:T(8,128)}, f32[256,128]{1,0:T(8,128)S(1)}, u32[]{:S(2)}, u32[]{:S(2)}) collective-permute-start(f32[256,128]{1,0:T(8,128)} %get-tuple-element.18), channel_id=1, source_target_pairs={{0,12},{4,8},{8,4},{12,0},{1,13},{5,9},{9,5},{13,1},{2,14},{6,10},... | collective-permute-start | bytes 393224 | tf_op jit(solution)/shard_map/ppermute | solution.py:315
  107.3 0.0 collective-permute-done.8.refs_2_
  107.3 1.5 %collective-permute-start.4 = (f32[256,128]{1,0:T(8,128)}, f32[256,128]{1,0:T(8,128)S(1)}, u32[]{:S(2)}, u32[]{:S(2)}) collective-permute-start(f32[256,128]{1,0:T(8,128)} %get-tuple-element.19), channel_id=1, source_target_pairs={{0,8},{4,12},{8,0},{12,4},{1,9},{5,13},{9,1},{13,5},{2,10},{6,14},... | collective-permute-start | bytes 393224 | tf_op jit(solution)/shard_map/ppermute | solution.py:315
  108.7 8.9 %attend.4 = (f32[256,128]{1,0:T(8,128)}, f32[256,128]{1,0:T(8,128)}, f32[256,128]{1,0:T(8,128)}, f32[256,128]{1,0:T(8,128)}) custom-call(s32[1,1024]{1,0:T(1,128)} %bitcast.14, s32[1024,1]{1,0:T(8,128)} %copy.5.place_col_ref, f32[768,128]{1,0:T(8,128)} %collective-permute-done.6.refs_0_, f32[768,128]{1,0:T(8,128)} %collective-permute-done.7.refs_1_, ...), custom_call_target="tpu_custom_call" | custom-call | flops 3953131520 | bytes 2097152 | tf_op jit(solution)/shard_map/attend/pallas_call | solution.py:292
  117.6 0.0 collective-permute-done.10.refs_1_
  117.6 0.5 collective-permute-start.5
  118.1 0.0 collective-permute-done.11.refs_2_
  118.1 1.6 %collective-permute-start.12 = (f32[256,128]{1,0:T(8,128)}, f32[256,128]{1,0:T(8,128)S(1)}, u32[]{:S(2)}, u32[]{:S(2)}) collective-permute-start(f32[256,128]{1,0:T(8,128)} %get-tuple-element.23), channel_id=1, source_target_pairs={{0,4},{4,0},{8,12},{12,8},{1,5},{5,1},{9,13},{13,9},{2,6},{6,2},{1... | collective-permute-start | bytes 393224 | tf_op jit(solution)/shard_map/ppermute | solution.py:315
  119.7 0.0 collective-permute-done.9.refs_0_
  119.7 1.4 collective-permute-start.13
  121.2 8.7 %attend.5 = (f32[256,128]{1,0:T(8,128)}, f32[256,128]{1,0:T(8,128)}, f32[256,128]{1,0:T(8,128)}, f32[256,128]{1,0:T(8,128)}) custom-call(s32[1,1024]{1,0:T(1,128)} %bitcast.15, s32[1024,1]{1,0:T(8,128)} %copy.5.place_col_ref, f32[768,128]{1,0:T(8,128)} %copy-done.13, f32[768,128]{1,0:T(8,128)} %copy-done.12, f32[768,128]{1,0:T(8,128)} %collective-permute-done.11.refs_2_, ...), custom_call_target="tpu_custom_call" | custom-call | flops 3953131520 | bytes 2097152 | tf_op jit(solution)/shard_map/attend/pallas_call | solution.py:292
  129.9 0.0 collective-permute-done.3.refs_1_
  129.9 1.4 collective-permute-start.14
  131.4 0.0 collective-permute-done.4.refs_2_
  131.4 0.7 collective-permute-start.15
  132.1 0.0 collective-permute-done.5.refs_3_
  132.1 1.9 %collective-permute-start.16 = (f32[256,128]{1,0:T(8,128)}, f32[256,128]{1,0:T(8,128)S(1)}, u32[]{:S(2)}, u32[]{:S(2)}) collective-permute-start(f32[256,128]{1,0:T(8,128)} %get-tuple-element.27), channel_id=1, source_target_pairs={{0,12},{4,8},{8,4},{12,0},{1,13},{5,9},{9,5},{13,1},{2,14},{6,10},... | collective-permute-start | bytes 393224 | tf_op jit(solution)/shard_map/ppermute | solution.py:315
  133.9 2.1 %put_blocks.1 = f32[256,1536]{1,0:T(8,128)} custom-call(f32[256,128]{1,0:T(8,128)} %get-tuple-element.17.refs_0_, f32[256,128]{1,0:T(8,128)} %copy-done.4, f32[256,128]{1,0:T(8,128)} %copy-done.5, f32[256,128]{1,0:T(8,128)} %copy-done.6, f32[256,128]{1,0:T(8,128)} %get-tuple-element.21.refs_4_, f32[256,128]{1,0:T(8,128)} %get-tuple-element.22.refs_5_), custom_call_target="tpu_custom_call" | custom-call | bytes 1572864 | tf_op jit(solution)/shard_map/put_blocks/pallas_call | solution.py:190
  136.1 0.0 collective-permute-done.12
  136.1 1.2 collective-permute-start.17
  137.3 0.7 constant_dynamic-update-slice_fusion.5
  137.9 0.0 collective-permute-done.13
  137.9 0.7 constant_dynamic-update-slice_fusion.4
  138.6 0.0 collective-permute-done.14
  138.6 0.7 constant_dynamic-update-slice_fusion.3
  139.3 0.0 collective-permute-done.15
  139.3 0.7 constant_dynamic-update-slice_fusion.2
  139.9 1.1 collective-permute-done.16
  141.1 0.7 constant_dynamic-update-slice_fusion.1
  141.8 4.3 %collective-permute-done.17 = f32[256,128]{1,0:T(8,128)S(1)} collective-permute-done((f32[256,128]{1,0:T(8,128)S(1)}, f32[256,128]{1,0:T(8,128)S(1)}, u32[]{:S(2)}, u32[]{:S(2)}) %collective-permute-start.17) | collective-permute-done | bytes 131104 | tf_op jit(solution)/shard_map/ppermute | solution.py:315
  146.1 0.7 constant_dynamic-update-slice_fusion
  (33 shorter events, 0.1 us)
Async XLA Ops:
  1.8 30.7 %collective-permute-start.2 = (f32[776,128]{1,0:T(8,128)}, f32[776,128]{1,0:T(8,128)S(1)}, u32[]{:S(2)}, u32[]{:S(2)}) collective-permute-start(f32[776,128]{1,0:T(8,128)} %pack.14), channel_id=1, source_target_pairs={{0,4},{4,0},{8,12},{12,8},{1,5},{5,1},{9,13},{13,9},{2,6},{6,2},{1... | collective-permute-start | bytes 1191944 | tf_op jit(solution)/shard_map/ppermute | solution.py:315
  6.8 38.7 %collective-permute-start.1 = (f32[776,128]{1,0:T(8,128)}, f32[776,128]{1,0:T(8,128)S(1)}, u32[]{:S(2)}, u32[]{:S(2)}) collective-permute-start(f32[776,128]{1,0:T(8,128)} %pack.13), channel_id=1, source_target_pairs={{0,8},{4,12},{8,0},{12,4},{1,9},{5,13},{9,1},{13,5},{2,10},{6,14},... | collective-permute-start | bytes 1191944 | tf_op jit(solution)/shard_map/ppermute | solution.py:315
  11.3 34.3 %collective-permute-start = (f32[776,128]{1,0:T(8,128)}, f32[776,128]{1,0:T(8,128)S(1)}, u32[]{:S(2)}, u32[]{:S(2)}) collective-permute-start(f32[776,128]{1,0:T(8,128)} %pack.12), channel_id=1, source_target_pairs={{0,12},{4,8},{8,4},{12,0},{1,13},{5,9},{9,5},{13,1},{2,14},{6,10},... | collective-permute-start | bytes 1191944 | tf_op jit(solution)/shard_map/ppermute | solution.py:315
  13.2 104.4 %collective-permute-start.10 = (f32[768,128]{1,0:T(8,128)}, f32[768,128]{1,0:T(8,128)S(1)}, u32[]{:S(2)}, u32[]{:S(2)}) collective-permute-start(f32[768,128]{1,0:T(8,128)} %pack.21), channel_id=1, source_target_pairs={{0,8},{4,12},{8,0},{12,4},{1,9},{5,13},{9,1},{13,5},{2,10},{6,14},... | collective-permute-start | bytes 1179656 | tf_op jit(solution)/shard_map/ppermute | solution.py:315
  17.0 101.1 %collective-permute-start.11 = (f32[768,128]{1,0:T(8,128)}, f32[768,128]{1,0:T(8,128)}, u32[]{:S(2)}, u32[]{:S(2)}) collective-permute-start(f32[768,128]{1,0:T(8,128)} %pack.22), channel_id=1, source_target_pairs={{0,4},{4,0},{8,12},{12,8},{1,5},{5,1},{9,13},{13,9},{2,6},{6,2},{1... | collective-permute-start | bytes 1179656 | tf_op jit(solution)/shard_map/ppermute | solution.py:315
  30.5 2.1 %copy-start.3 = (f32[768,128]{1,0:T(8,128)S(1)}, f32[768,128]{1,0:T(8,128)}, u32[]{:S(2)}) copy-start(f32[768,128]{1,0:T(8,128)} %pack.16) | copy-start | bytes 1179652
  30.5 15.0 %copy-start.2 = (f32[768,128]{1,0:T(8,128)S(1)}, f32[768,128]{1,0:T(8,128)}, u32[]{:S(2)}) copy-start(f32[768,128]{1,0:T(8,128)} %pack.17) | copy-start | bytes 1179652
  30.6 15.0 %copy-start.1 = (f32[768,128]{1,0:T(8,128)S(1)}, f32[768,128]{1,0:T(8,128)}, u32[]{:S(2)}) copy-start(f32[768,128]{1,0:T(8,128)} %pack.18) | copy-start | bytes 1179652
  30.6 40.9 %copy-start.7 = (s32[256]{0:T(256)S(1)}, s32[256]{0:T(256)}, u32[]{:S(2)}) copy-start(s32[256]{0:T(256)} %param.7) | copy-start | bytes 3076
  30.6 42.0 %copy-start = (f32[768,128]{1,0:T(8,128)S(1)}, f32[768,128]{1,0:T(8,128)}, u32[]{:S(2)}) copy-start(f32[768,128]{1,0:T(8,128)} %pack.20) | copy-start | bytes 1179652
  32.6 42.4 %copy-start.9 = (f32[776,128]{1,0:T(8,128)}, f32[776,128]{1,0:T(8,128)S(1)}, u32[]{:S(2)}) copy-start(f32[776,128]{1,0:T(8,128)S(1)} %collective-permute-done.2.refs_2_) | copy-start | bytes 1191940
  32.6 40.0 %collective-permute-start.6 = (f32[768,128]{1,0:T(8,128)S(1)}, f32[768,128]{1,0:T(8,128)}, u32[]{:S(2)}, u32[]{:S(2)}) collective-permute-start(f32[768,128]{1,0:T(8,128)S(1)} %copy-done.3), channel_id=1, source_target_pairs={{0,12},{4,8},{8,4},{12,0},{1,13},{5,9},{9,5},{13,1},{2,14},{6,10},... | collective-permute-start | bytes 1179656 | tf_op jit(solution)/shard_map/ppermute | solution.py:315
  45.6 29.5 %copy-start.10 = (f32[776,128]{1,0:T(8,128)}, f32[776,128]{1,0:T(8,128)S(1)}, u32[]{:S(2)}) copy-start(f32[776,128]{1,0:T(8,128)S(1)} %collective-permute-done.1.refs_1_) | copy-start | bytes 1191940
  45.6 59.2 %collective-permute-start.7 = (f32[768,128]{1,0:T(8,128)S(1)}, f32[768,128]{1,0:T(8,128)}, u32[]{:S(2)}, u32[]{:S(2)}) collective-permute-start(f32[768,128]{1,0:T(8,128)S(1)} %copy-done.2), channel_id=1, source_target_pairs={{0,8},{4,12},{8,0},{12,4},{1,9},{5,13},{9,1},{13,5},{2,10},{6,14},... | collective-permute-start | bytes 1179656 | tf_op jit(solution)/shard_map/ppermute | solution.py:315
  45.6 29.4 %copy-start.11 = (f32[776,128]{1,0:T(8,128)}, f32[776,128]{1,0:T(8,128)S(1)}, u32[]{:S(2)}) copy-start(f32[776,128]{1,0:T(8,128)S(1)} %collective-permute-done.refs_0_) | copy-start | bytes 1191940
  45.6 61.6 %collective-permute-start.8 = (f32[768,128]{1,0:T(8,128)S(1)}, f32[768,128]{1,0:T(8,128)}, u32[]{:S(2)}, u32[]{:S(2)}) collective-permute-start(f32[768,128]{1,0:T(8,128)S(1)} %copy-done.1), channel_id=1, source_target_pairs={{0,4},{4,0},{8,12},{12,8},{1,5},{5,1},{9,13},{13,9},{2,6},{6,2},{1... | collective-permute-start | bytes 1179656 | tf_op jit(solution)/shard_map/ppermute | solution.py:315
  71.5 3.5 %copy-start.8 = (s32[1024]{0:T(1024)}, s32[1024]{0:T(1024)S(1)}, u32[]{:S(2)}) copy-start(s32[1024]{0:T(1024)S(1)} %pad_add_fusion) | copy-start | bytes 12292
  72.6 47.2 %collective-permute-start.9 = (f32[768,128]{1,0:T(8,128)S(1)}, f32[768,128]{1,0:T(8,128)S(1)}, u32[]{:S(2)}, u32[]{:S(2)}) collective-permute-start(f32[768,128]{1,0:T(8,128)S(1)} %copy-done), channel_id=1, source_target_pairs={{0,12},{4,8},{8,4},{12,0},{1,13},{5,9},{9,5},{13,1},{2,14},{6,10},... | collective-permute-start | bytes 1179656 | tf_op jit(solution)/shard_map/ppermute | solution.py:315
  104.8 25.1 %collective-permute-start.3 = (f32[256,128]{1,0:T(8,128)}, f32[256,128]{1,0:T(8,128)S(1)}, u32[]{:S(2)}, u32[]{:S(2)}) collective-permute-start(f32[256,128]{1,0:T(8,128)} %get-tuple-element.18), channel_id=1, source_target_pairs={{0,12},{4,8},{8,4},{12,0},{1,13},{5,9},{9,5},{13,1},{2,14},{6,10},... | collective-permute-start | bytes 393224 | tf_op jit(solution)/shard_map/ppermute | solution.py:315
  107.3 10.4 %copy-start.16 = (f32[256,128]{1,0:T(8,128)S(1)}, f32[256,128]{1,0:T(8,128)}, u32[]{:S(2)}) copy-start(f32[256,128]{1,0:T(8,128)} %get-tuple-element.20) | copy-start | bytes 393220
  107.3 24.1 %collective-permute-start.4 = (f32[256,128]{1,0:T(8,128)}, f32[256,128]{1,0:T(8,128)S(1)}, u32[]{:S(2)}, u32[]{:S(2)}) collective-permute-start(f32[256,128]{1,0:T(8,128)} %get-tuple-element.19), channel_id=1, source_target_pairs={{0,8},{4,12},{8,0},{12,4},{1,9},{5,13},{9,1},{13,5},{2,10},{6,14},... | collective-permute-start | bytes 393224 | tf_op jit(solution)/shard_map/ppermute | solution.py:315
  117.6 3.6 %copy-start.12 = (f32[768,128]{1,0:T(8,128)}, f32[768,128]{1,0:T(8,128)S(1)}, u32[]{:S(2)}) copy-start(f32[768,128]{1,0:T(8,128)S(1)} %collective-permute-done.10.refs_1_) | copy-start | bytes 1179652
  117.6 14.4 %collective-permute-start.5 = (f32[256,128]{1,0:T(8,128)S(1)}, f32[256,128]{1,0:T(8,128)S(1)}, u32[]{:S(2)}, u32[]{:S(2)}) collective-permute-start(f32[256,128]{1,0:T(8,128)S(1)} %copy-done.16), channel_id=1, source_target_pairs={{0,4},{4,0},{8,12},{12,8},{1,5},{5,1},{9,13},{13,9},{2,6},{6,2},{1... | collective-permute-start | bytes 393224 | tf_op jit(solution)/shard_map/ppermute | solution.py:315
  118.1 17.9 %collective-permute-start.12 = (f32[256,128]{1,0:T(8,128)}, f32[256,128]{1,0:T(8,128)S(1)}, u32[]{:S(2)}, u32[]{:S(2)}) collective-permute-start(f32[256,128]{1,0:T(8,128)} %get-tuple-element.23), channel_id=1, source_target_pairs={{0,4},{4,0},{8,12},{12,8},{1,5},{5,1},{9,13},{13,9},{2,6},{6,2},{1... | collective-permute-start | bytes 393224 | tf_op jit(solution)/shard_map/ppermute | solution.py:315
  119.7 1.5 copy-start.13
  119.7 10.2 %copy-start.14 = (f32[256,128]{1,0:T(8,128)S(1)}, f32[256,128]{1,0:T(8,128)}, u32[]{:S(2)}) copy-start(f32[256,128]{1,0:T(8,128)} %get-tuple-element.25) | copy-start | bytes 393220
  119.7 18.2 %collective-permute-start.13 = (f32[256,128]{1,0:T(8,128)}, f32[256,128]{1,0:T(8,128)S(1)}, u32[]{:S(2)}, u32[]{:S(2)}) collective-permute-start(f32[256,128]{1,0:T(8,128)} %get-tuple-element.24), channel_id=1, source_target_pairs={{0,8},{4,12},{8,0},{12,4},{1,9},{5,13},{9,1},{13,5},{2,10},{6,14},... | collective-permute-start | bytes 393224 | tf_op jit(solution)/shard_map/ppermute | solution.py:315
  129.9 6.2 %copy-start.15 = (f32[256,128]{1,0:T(8,128)S(1)}, f32[256,128]{1,0:T(8,128)}, u32[]{:S(2)}) copy-start(f32[256,128]{1,0:T(8,128)} %get-tuple-element.28) | copy-start | bytes 393220
  129.9 4.0 %copy-start.4 = (f32[256,128]{1,0:T(8,128)}, f32[256,128]{1,0:T(8,128)S(1)}, u32[]{:S(2)}) copy-start(f32[256,128]{1,0:T(8,128)S(1)} %collective-permute-done.3.refs_1_) | copy-start | bytes 393220
  129.9 8.7 %collective-permute-start.14 = (f32[256,128]{1,0:T(8,128)S(1)}, f32[256,128]{1,0:T(8,128)S(1)}, u32[]{:S(2)}, u32[]{:S(2)}) collective-permute-start(f32[256,128]{1,0:T(8,128)S(1)} %copy-done.14), channel_id=1, source_target_pairs={{0,12},{4,8},{8,4},{12,0},{1,13},{5,9},{9,5},{13,1},{2,14},{6,10},... | collective-permute-start | bytes 393224 | tf_op jit(solution)/shard_map/ppermute | solution.py:315
  131.4 2.6 %copy-start.5 = (f32[256,128]{1,0:T(8,128)}, f32[256,128]{1,0:T(8,128)S(1)}, u32[]{:S(2)}) copy-start(f32[256,128]{1,0:T(8,128)S(1)} %collective-permute-done.4.refs_2_) | copy-start | bytes 393220
  131.4 7.9 %collective-permute-start.15 = (f32[256,128]{1,0:T(8,128)}, f32[256,128]{1,0:T(8,128)S(1)}, u32[]{:S(2)}, u32[]{:S(2)}) collective-permute-start(f32[256,128]{1,0:T(8,128)} %get-tuple-element.26), channel_id=1, source_target_pairs={{0,4},{4,0},{8,12},{12,8},{1,5},{5,1},{9,13},{13,9},{2,6},{6,2},{1... | collective-permute-start | bytes 393224 | tf_op jit(solution)/shard_map/ppermute | solution.py:315
  132.1 1.9 %copy-start.6 = (f32[256,128]{1,0:T(8,128)}, f32[256,128]{1,0:T(8,128)S(1)}, u32[]{:S(2)}) copy-start(f32[256,128]{1,0:T(8,128)S(1)} %collective-permute-done.5.refs_3_) | copy-start | bytes 393220
  132.1 9.0 %collective-permute-start.16 = (f32[256,128]{1,0:T(8,128)}, f32[256,128]{1,0:T(8,128)S(1)}, u32[]{:S(2)}, u32[]{:S(2)}) collective-permute-start(f32[256,128]{1,0:T(8,128)} %get-tuple-element.27), channel_id=1, source_target_pairs={{0,12},{4,8},{8,4},{12,0},{1,13},{5,9},{9,5},{13,1},{2,14},{6,10},... | collective-permute-start | bytes 393224 | tf_op jit(solution)/shard_map/ppermute | solution.py:315
  136.1 10.0 %collective-permute-start.17 = (f32[256,128]{1,0:T(8,128)S(1)}, f32[256,128]{1,0:T(8,128)S(1)}, u32[]{:S(2)}, u32[]{:S(2)}) collective-permute-start(f32[256,128]{1,0:T(8,128)S(1)} %copy-done.15), channel_id=1, source_target_pairs={{0,8},{4,12},{8,0},{12,4},{1,9},{5,13},{9,1},{13,5},{2,10},{6,14},... | collective-permute-start | bytes 393224 | tf_op jit(solution)/shard_map/ppermute | solution.py:315

commit v2 on v1

--- a/solution.py
+++ b/solution.py
@@ -109,15 +109,15 @@
     return returned.reshape(-1, col_width)[slot_index]
 
 
+TERMS = (3, 3, 2)
+
+
 def split_terms(x, count):
     terms = []
     for _ in range(count):
         terms.append(x.astype(jnp.bfloat16))
         x = x - terms[-1].astype(jnp.float32)
     return terms
-
-
-TERMS = (3, 3, 2)
 
 
 def pack_kernel(flip, head, per_window, tailed, *refs):
@@ -166,15 +166,16 @@
     )(*sources, *extra)
 
 
-def place_kernel(head, per_window, peers, *refs):
-    blocks = refs[:len(peers)]
-    result_ref, landed = refs[-2:]
+def put_kernel(spots, per_window, *refs):
+    blocks, result_ref, landed = refs[: len(spots)], refs[-2], refs[-1]
     copies = []
-    for n, (block, flip) in enumerate(zip(blocks, peers)):
+    for n, (flip, head) in enumerate(spots):
         peer = lax.axis_index("win") ^ flip
-        first = pl.multiple_of((peer * per_window + head[n]) * HEAD_DIM, HEAD_DIM)
+        first = pl.multiple_of((peer * per_window + head) * HEAD_DIM, HEAD_DIM)
         copies.append(
-            pltpu.make_async_copy(block, result_ref.at[:, pl.ds(first, HEAD_DIM)], landed.at[n])
+            pltpu.make_async_copy(
+                blocks[n], result_ref.at[:, pl.ds(first, HEAD_DIM)], landed.at[n]
+            )
         )
     for copy in copies:
         copy.start()
@@ -182,23 +183,20 @@
         copy.wait()
 
 
-def put_blocks(entries, per_window, result_shape, result=None):
-    blocks = [entry[2] for entry in entries]
-    flips, heads = [entry[0] for entry in entries], [entry[1] for entry in entries]
-    anywhere = pl.BlockSpec(memory_space=pl.ANY)
-    extra = [] if result is None else [result]
+def put_blocks(entries, per_window, col_width):
+    blocks = [block for _, _, block in entries]
+    spots = [(flip, head) for flip, head, _ in entries]
     return pl.pallas_call(
-        functools.partial(place_kernel, heads, per_window, flips),
-        in_specs=[pl.BlockSpec(memory_space=pltpu.VMEM)] * len(blocks) + [anywhere] * len(extra),
-        out_specs=anywhere,
-        out_shape=result_shape,
-        input_output_aliases={len(blocks): 0} if extra else {},
+        functools.partial(put_kernel, spots, per_window),
+        in_specs=[pl.BlockSpec(memory_space=pltpu.VMEM)] * len(blocks),
+        out_specs=pl.BlockSpec(memory_space=pl.ANY),
+        out_shape=jax.ShapeDtypeStruct((blocks[0].shape[0], col_width), jnp.float32),
         scratch_shapes=[pltpu.SemaphoreType.DMA((len(blocks),))],
         cost_estimate=pl.CostEstimate(
             flops=0, transcendentals=0, bytes_accessed=8 * blocks[0].size * len(blocks)
         ),
         name="put_blocks",
-    )(*blocks, *extra)
+    )(*blocks)
 
 
 def attend_kernel(peers, place_row_ref, place_col_ref, *refs):
@@ -329,16 +327,15 @@
         + [merge_target]
     )
     place_row, place_col = place[None, :], place[:, None]
-    result_shape = jax.ShapeDtypeStruct((rows, col_width), jnp.float32)
     early, late = [], []
     for head in range(per_window):
         blocks = attend(place_row, place_col, arrived[head] + [own[head]])
         early.append((0, head, blocks[-1]))
         for flip, block in zip(flips, blocks):
             (early if head == 0 else late).append((flip, head, swap(block, flip)))
-    result = put_blocks(early, per_window, result_shape)
+    result = put_blocks(early, per_window, col_width)
     window = lax.axis_index("win")
-    for flip, head, block in (*late[2:3], *late[1::-1], late[5], *late[3:5]):
+    for flip, head, block in sorted(late, key=lambda entry: (entry[1], entry[0] > 1, -entry[0])):
         result = lax.dynamic_update_slice_in_dim(
             result, block, ((window ^ flip) * per_window + head) * HEAD_DIM, 1
         )

time: 147 us -> 147 us (level)
  no operation moved by 1% of the time
where the time goes in v2:
time: 147 us
  starting transfers between devices  50.9 us (35%)
  Pallas kernels  50.5 us (34%)
  waiting for transfers between devices  40 us (27%)
  local copies, waits for them, and re-layouts  5.08 us (3%)
    ppermute x18, starting transfers between devices, swap(): return lax.ppermute(x, 'win', [(n, n ^ flip) for n in range(window_count)])  50.9 us
    ppermute x18, waiting for transfers between devices, swap(): return lax.ppermute(x, 'win', [(n, n ^ flip) for n in range(window_count)])  40 us
    pallas_call x3, Pallas kernels, attend(): pl.pallas_call(functools.partial(attend_kernel, peers), in_specs=[pl.Bloc...  26.3 us
    pallas_call x12, Pallas kernels, pack(): pl.pallas_call(functools.partial(pack_kernel, flip, head, per_window, tai...  22 us
    dynamic_update_slice x6, local copies, waits for them, and re-layouts, by_heads(): lax.dynamic_update_slice_in_dim(result, block, ((window ^ flip) * per_win...  3.98 us
  transfers between devices with their start and end apart: 18, of which 4 were waited for; matrix products, arithmetic and copies ran while one was open for 3% of the time, Pallas kernels for 33%

profile of v2, /device:TPU:0, one launch (start us, length us, event | category | flops | bytes accessed | tf_op | source)
XLA Modules:
  0.0 146.8 jit_solution(1940274889897688457)
XLA Ops:
  0.0 1.8 %pack.14 = f32[776,128]{1,0:T(8,128)} custom-call(f32[256,1536]{1,0:T(8,128)} %refs_0_.23, f32[256,1536]{1,0:T(8,128)} %refs_1_.23, f32[256,1536]{1,0:T(8,128)} %refs_2_.23, s32[2,128]{1,0:T(2,128)} %bitcast.9), custom_call_target="tpu_custom_call" | custom-call | bytes 794624 | tf_op jit(solution)/shard_map/pack/pallas_call | solution.py:155
  1.8 3.1 %collective-permute-start.2 = (f32[776,128]{1,0:T(8,128)}, f32[776,128]{1,0:T(8,128)S(1)}, u32[]{:S(2)}, u32[]{:S(2)}) collective-permute-start(f32[776,128]{1,0:T(8,128)} %pack.14), channel_id=1, source_target_pairs={{0,4},{4,0},{8,12},{12,8},{1,5},{5,1},{9,13},{13,9},{2,6},{6,2},{1... | collective-permute-start | bytes 1191944 | tf_op jit(solution)/shard_map/ppermute | solution.py:313
  5.0 1.8 %pack.13 = f32[776,128]{1,0:T(8,128)} custom-call(f32[256,1536]{1,0:T(8,128)} %refs_0_.23, f32[256,1536]{1,0:T(8,128)} %refs_1_.23, f32[256,1536]{1,0:T(8,128)} %refs_2_.23, s32[2,128]{1,0:T(2,128)} %bitcast.10), custom_call_target="tpu_custom_call" | custom-call | bytes 794624 | tf_op jit(solution)/shard_map/pack/pallas_call | solution.py:155
  6.8 2.7 %collective-permute-start.1 = (f32[776,128]{1,0:T(8,128)}, f32[776,128]{1,0:T(8,128)S(1)}, u32[]{:S(2)}, u32[]{:S(2)}) collective-permute-start(f32[776,128]{1,0:T(8,128)} %pack.13), channel_id=1, source_target_pairs={{0,8},{4,12},{8,0},{12,4},{1,9},{5,13},{9,1},{13,5},{2,10},{6,14},... | collective-permute-start | bytes 1191944 | tf_op jit(solution)/shard_map/ppermute | solution.py:313
  9.5 1.8 %pack.12 = f32[776,128]{1,0:T(8,128)} custom-call(f32[256,1536]{1,0:T(8,128)} %refs_0_.23, f32[256,1536]{1,0:T(8,128)} %refs_1_.23, f32[256,1536]{1,0:T(8,128)} %refs_2_.23, s32[2,128]{1,0:T(2,128)} %bitcast.11), custom_call_target="tpu_custom_call" | custom-call | bytes 794624 | tf_op jit(solution)/shard_map/pack/pallas_call | solution.py:155
  11.3 0.1 collective-permute-start
  11.4 1.8 %pack.21 = f32[768,128]{1,0:T(8,128)} custom-call(f32[256,1536]{1,0:T(8,128)} %refs_0_.23, f32[256,1536]{1,0:T(8,128)} %refs_1_.23, f32[256,1536]{1,0:T(8,128)} %refs_2_.23), custom_call_target="tpu_custom_call" | custom-call | bytes 786432 | tf_op jit(solution)/shard_map/pack/pallas_call | solution.py:155
  13.2 1.9 %collective-permute-start.10 = (f32[768,128]{1,0:T(8,128)}, f32[768,128]{1,0:T(8,128)S(1)}, u32[]{:S(2)}, u32[]{:S(2)}) collective-permute-start(f32[768,128]{1,0:T(8,128)} %pack.21), channel_id=1, source_target_pairs={{0,8},{4,12},{8,0},{12,4},{1,9},{5,13},{9,1},{13,5},{2,10},{6,14},... | collective-permute-start | bytes 1179656 | tf_op jit(solution)/shard_map/ppermute | solution.py:313
  15.2 1.8 %pack.22 = f32[768,128]{1,0:T(8,128)} custom-call(f32[256,1536]{1,0:T(8,128)} %refs_0_.23, f32[256,1536]{1,0:T(8,128)} %refs_1_.23, f32[256,1536]{1,0:T(8,128)} %refs_2_.23), custom_call_target="tpu_custom_call" | custom-call | bytes 786432 | tf_op jit(solution)/shard_map/pack/pallas_call | solution.py:155
  17.0 2.5 %collective-permute-start.11 = (f32[768,128]{1,0:T(8,128)}, f32[768,128]{1,0:T(8,128)}, u32[]{:S(2)}, u32[]{:S(2)}) collective-permute-start(f32[768,128]{1,0:T(8,128)} %pack.22), channel_id=1, source_target_pairs={{0,4},{4,0},{8,12},{12,8},{1,5},{5,1},{9,13},{13,9},{2,6},{6,2},{1... | collective-permute-start | bytes 1179656 | tf_op jit(solution)/shard_map/ppermute | solution.py:313
  19.5 1.8 %pack.15.refs_3_ = f32[768,128]{1,0:T(8,128)} custom-call(f32[256,1536]{1,0:T(8,128)} %refs_0_.23, f32[256,1536]{1,0:T(8,128)} %refs_1_.23, f32[256,1536]{1,0:T(8,128)} %refs_2_.23), custom_call_target="tpu_custom_call" | custom-call | bytes 786432 | tf_op jit(solution)/shard_map/pack/pallas_call | solution.py:155
  21.4 1.8 %pack.20 = f32[768,128]{1,0:T(8,128)} custom-call(f32[256,1536]{1,0:T(8,128)} %refs_0_.23, f32[256,1536]{1,0:T(8,128)} %refs_1_.23, f32[256,1536]{1,0:T(8,128)} %refs_2_.23), custom_call_target="tpu_custom_call" | custom-call | bytes 786432 | tf_op jit(solution)/shard_map/pack/pallas_call | solution.py:155
  23.2 1.8 %pack.23.refs_3_ = f32[768,128]{1,0:T(8,128)} custom-call(f32[256,1536]{1,0:T(8,128)} %refs_0_.23, f32[256,1536]{1,0:T(8,128)} %refs_1_.23, f32[256,1536]{1,0:T(8,128)} %refs_2_.23), custom_call_target="tpu_custom_call" | custom-call | bytes 786432 | tf_op jit(solution)/shard_map/pack/pallas_call | solution.py:155
  25.1 1.8 %pack.16 = f32[768,128]{1,0:T(8,128)} custom-call(f32[256,1536]{1,0:T(8,128)} %refs_0_.23, f32[256,1536]{1,0:T(8,128)} %refs_1_.23, f32[256,1536]{1,0:T(8,128)} %refs_2_.23), custom_call_target="tpu_custom_call" | custom-call | bytes 786432 | tf_op jit(solution)/shard_map/pack/pallas_call | solution.py:155
  26.9 1.8 %pack.17 = f32[768,128]{1,0:T(8,128)} custom-call(f32[256,1536]{1,0:T(8,128)} %refs_0_.23, f32[256,1536]{1,0:T(8,128)} %refs_1_.23, f32[256,1536]{1,0:T(8,128)} %refs_2_.23), custom_call_target="tpu_custom_call" | custom-call | bytes 786432 | tf_op jit(solution)/shard_map/pack/pallas_call | solution.py:155
  28.7 1.8 %pack.18 = f32[768,128]{1,0:T(8,128)} custom-call(f32[256,1536]{1,0:T(8,128)} %refs_0_.23, f32[256,1536]{1,0:T(8,128)} %refs_1_.23, f32[256,1536]{1,0:T(8,128)} %refs_2_.23), custom_call_target="tpu_custom_call" | custom-call | bytes 786432 | tf_op jit(solution)/shard_map/pack/pallas_call | solution.py:155
  30.5 0.0 copy-start.3
  30.5 0.0 copy-start.2
  30.6 0.0 copy-start.1
  30.6 0.0 copy-start.7
  30.6 1.9 %pack.19.refs_3_ = f32[768,128]{1,0:T(8,128)} custom-call(f32[256,1536]{1,0:T(8,128)} %refs_0_.23, f32[256,1536]{1,0:T(8,128)} %refs_1_.23, f32[256,1536]{1,0:T(8,128)} %refs_2_.23), custom_call_target="tpu_custom_call" | custom-call | bytes 786432 | tf_op jit(solution)/shard_map/pack/pallas_call | solution.py:155
  32.6 0.0 collective-permute-done.2.refs_2_
  32.6 0.1 collective-permute-start.6
  32.7 12.9 %collective-permute-done.1.refs_1_ = f32[776,128]{1,0:T(8,128)S(1)} collective-permute-done((f32[776,128]{1,0:T(8,128)}, f32[776,128]{1,0:T(8,128)S(1)}, u32[]{:S(2)}, u32[]{:S(2)}) %collective-permute-start.1) | collective-permute-done | bytes 397344 | tf_op jit(solution)/shard_map/ppermute | solution.py:313
  45.6 0.0 collective-permute-start.7
  45.6 0.0 collective-permute-done.refs_0_
  45.6 25.9 %collective-permute-start.8 = (f32[768,128]{1,0:T(8,128)S(1)}, f32[768,128]{1,0:T(8,128)}, u32[]{:S(2)}, u32[]{:S(2)}) collective-permute-start(f32[768,128]{1,0:T(8,128)S(1)} %copy-done.1), channel_id=1, source_target_pairs={{0,4},{4,0},{8,12},{12,8},{1,5},{5,1},{9,13},{13,9},{2,6},{6,2},{1... | collective-permute-start | bytes 1179656 | tf_op jit(solution)/shard_map/ppermute | solution.py:313
  71.5 1.0 copy.5.place_col_ref
  72.6 0.0 collective-permute-done.6.refs_0_
  72.6 2.5 %collective-permute-start.9 = (f32[768,128]{1,0:T(8,128)S(1)}, f32[768,128]{1,0:T(8,128)S(1)}, u32[]{:S(2)}, u32[]{:S(2)}) collective-permute-start(f32[768,128]{1,0:T(8,128)S(1)} %copy-done), channel_id=1, source_target_pairs={{0,12},{4,8},{8,4},{12,0},{1,13},{5,9},{9,5},{13,1},{2,14},{6,10},... | collective-permute-start | bytes 1179656 | tf_op jit(solution)/shard_map/ppermute | solution.py:313
  75.0 0.0 copy-done.9
  75.1 8.8 %attend.3 = (f32[256,128]{1,0:T(8,128)}, f32[256,128]{1,0:T(8,128)}, f32[256,128]{1,0:T(8,128)}, f32[256,128]{1,0:T(8,128)}) custom-call(s32[1,1024]{1,0:T(1,128)} %bitcast.13, s32[1024,1]{1,0:T(8,128)} %copy.5.place_col_ref, f32[776,128]{1,0:T(8,128)} %copy-done.11, f32[776,128]{1,0:T(8,128)} %copy-done.10, f32[776,128]{1,0:T(8,128)} %copy-done.9, ...), custom_call_target="tpu_custom_call" | custom-call | flops 3953131520 | bytes 2097152 | tf_op jit(solution)/shard_map/attend/pallas_call | solution.py:290
  83.8 21.0 %collective-permute-done.7.refs_1_ = f32[768,128]{1,0:T(8,128)} collective-permute-done((f32[768,128]{1,0:T(8,128)S(1)}, f32[768,128]{1,0:T(8,128)}, u32[]{:S(2)}, u32[]{:S(2)}) %collective-permute-start.7) | collective-permute-done | bytes 393248 | tf_op jit(solution)/shard_map/ppermute | solution.py:313
  104.8 2.5 %collective-permute-start.3 = (f32[256,128]{1,0:T(8,128)}, f32[256,128]{1,0:T(8,128)S(1)}, u32[]{:S(2)}, u32[]{:S(2)}) collective-permute-start(f32[256,128]{1,0:T(8,128)} %get-tuple-element.18), channel_id=1, source_target_pairs={{0,12},{4,8},{8,4},{12,0},{1,13},{5,9},{9,5},{13,1},{2,14},{6,10},... | collective-permute-start | bytes 393224 | tf_op jit(solution)/shard_map/ppermute | solution.py:313
  107.3 0.0 collective-permute-done.8.refs_2_
  107.3 1.5 %collective-permute-start.4 = (f32[256,128]{1,0:T(8,128)}, f32[256,128]{1,0:T(8,128)S(1)}, u32[]{:S(2)}, u32[]{:S(2)}) collective-permute-start(f32[256,128]{1,0:T(8,128)} %get-tuple-element.19), channel_id=1, source_target_pairs={{0,8},{4,12},{8,0},{12,4},{1,9},{5,13},{9,1},{13,5},{2,10},{6,14},... | collective-permute-start | bytes 393224 | tf_op jit(solution)/shard_map/ppermute | solution.py:313
  108.7 8.9 %attend.4 = (f32[256,128]{1,0:T(8,128)}, f32[256,128]{1,0:T(8,128)}, f32[256,128]{1,0:T(8,128)}, f32[256,128]{1,0:T(8,128)}) custom-call(s32[1,1024]{1,0:T(1,128)} %bitcast.14, s32[1024,1]{1,0:T(8,128)} %copy.5.place_col_ref, f32[768,128]{1,0:T(8,128)} %collective-permute-done.6.refs_0_, f32[768,128]{1,0:T(8,128)} %collective-permute-done.7.refs_1_, ...), custom_call_target="tpu_custom_call" | custom-call | flops 3953131520 | bytes 2097152 | tf_op jit(solution)/shard_map/attend/pallas_call | solution.py:290
  117.6 0.0 collective-permute-done.10.refs_1_
  117.6 0.5 collective-permute-start.5
  118.1 0.0 collective-permute-done.11.refs_2_
  118.1 1.6 %collective-permute-start.12 = (f32[256,128]{1,0:T(8,128)}, f32[256,128]{1,0:T(8,128)S(1)}, u32[]{:S(2)}, u32[]{:S(2)}) collective-permute-start(f32[256,128]{1,0:T(8,128)} %get-tuple-element.23), channel_id=1, source_target_pairs={{0,4},{4,0},{8,12},{12,8},{1,5},{5,1},{9,13},{13,9},{2,6},{6,2},{1... | collective-permute-start | bytes 393224 | tf_op jit(solution)/shard_map/ppermute | solution.py:313
  119.7 0.0 collective-permute-done.9.refs_0_
  119.7 1.3 collective-permute-start.13
  121.1 8.7 %attend.5 = (f32[256,128]{1,0:T(8,128)}, f32[256,128]{1,0:T(8,128)}, f32[256,128]{1,0:T(8,128)}, f32[256,128]{1,0:T(8,128)}) custom-call(s32[1,1024]{1,0:T(1,128)} %bitcast.15, s32[1024,1]{1,0:T(8,128)} %copy.5.place_col_ref, f32[768,128]{1,0:T(8,128)} %copy-done.13, f32[768,128]{1,0:T(8,128)} %copy-done.12, f32[768,128]{1,0:T(8,128)} %collective-permute-done.11.refs_2_, ...), custom_call_target="tpu_custom_call" | custom-call | flops 3953131520 | bytes 2097152 | tf_op jit(solution)/shard_map/attend/pallas_call | solution.py:290
  129.8 0.0 collective-permute-done.3.refs_1_
  129.8 0.9 collective-permute-start.14
  130.7 0.0 collective-permute-done.4.refs_2_
  130.8 2.2 %collective-permute-start.15 = (f32[256,128]{1,0:T(8,128)}, f32[256,128]{1,0:T(8,128)S(1)}, u32[]{:S(2)}, u32[]{:S(2)}) collective-permute-start(f32[256,128]{1,0:T(8,128)} %get-tuple-element.26), channel_id=1, source_target_pairs={{0,4},{4,0},{8,12},{12,8},{1,5},{5,1},{9,13},{13,9},{2,6},{6,2},{1... | collective-permute-start | bytes 393224 | tf_op jit(solution)/shard_map/ppermute | solution.py:313
  133.0 0.0 collective-permute-done.5.refs_3_
  133.0 1.4 collective-permute-start.16
  134.3 2.1 %put_blocks.1 = f32[256,1536]{1,0:T(8,128)} custom-call(f32[256,128]{1,0:T(8,128)} %get-tuple-element.17.refs_0_, f32[256,128]{1,0:T(8,128)} %copy-done.4, f32[256,128]{1,0:T(8,128)} %copy-done.5, f32[256,128]{1,0:T(8,128)} %copy-done.6, f32[256,128]{1,0:T(8,128)} %get-tuple-element.21.refs_4_, f32[256,128]{1,0:T(8,128)} %get-tuple-element.22.refs_5_), custom_call_target="tpu_custom_call" | custom-call | bytes 1572864 | tf_op jit(solution)/shard_map/put_blocks/pallas_call | solution.py:189
  136.5 0.0 collective-permute-done.12
  136.5 0.3 collective-permute-start.17
  136.7 0.7 constant_dynamic-update-slice_fusion.5
  137.4 0.0 collective-permute-done.13
  137.4 0.7 constant_dynamic-update-slice_fusion.4
  138.1 4.7 %collective-permute-done.14 = f32[256,128]{1,0:T(8,128)S(1)} collective-permute-done((f32[256,128]{1,0:T(8,128)S(1)}, f32[256,128]{1,0:T(8,128)S(1)}, u32[]{:S(2)}, u32[]{:S(2)}) %collective-permute-start.14) | collective-permute-done | bytes 131104 | tf_op jit(solution)/shard_map/ppermute | solution.py:313
  142.8 0.7 constant_dynamic-update-slice_fusion.3
  143.5 0.0 collective-permute-done.15
  143.5 0.7 constant_dynamic-update-slice_fusion.2
  144.1 0.0 collective-permute-done.16
  144.1 0.7 constant_dynamic-update-slice_fusion.1
  144.8 1.4 collective-permute-done.17
  146.2 0.7 constant_dynamic-update-slice_fusion
  (33 shorter events, 0.1 us)
Async XLA Ops:
  1.8 30.7 %collective-permute-start.2 = (f32[776,128]{1,0:T(8,128)}, f32[776,128]{1,0:T(8,128)S(1)}, u32[]{:S(2)}, u32[]{:S(2)}) collective-permute-start(f32[776,128]{1,0:T(8,128)} %pack.14), channel_id=1, source_target_pairs={{0,4},{4,0},{8,12},{12,8},{1,5},{5,1},{9,13},{13,9},{2,6},{6,2},{1... | collective-permute-start | bytes 1191944 | tf_op jit(solution)/shard_map/ppermute | solution.py:313
  6.8 38.7 %collective-permute-start.1 = (f32[776,128]{1,0:T(8,128)}, f32[776,128]{1,0:T(8,128)S(1)}, u32[]{:S(2)}, u32[]{:S(2)}) collective-permute-start(f32[776,128]{1,0:T(8,128)} %pack.13), channel_id=1, source_target_pairs={{0,8},{4,12},{8,0},{12,4},{1,9},{5,13},{9,1},{13,5},{2,10},{6,14},... | collective-permute-start | bytes 1191944 | tf_op jit(solution)/shard_map/ppermute | solution.py:313
  11.3 34.3 %collective-permute-start = (f32[776,128]{1,0:T(8,128)}, f32[776,128]{1,0:T(8,128)S(1)}, u32[]{:S(2)}, u32[]{:S(2)}) collective-permute-start(f32[776,128]{1,0:T(8,128)} %pack.12), channel_id=1, source_target_pairs={{0,12},{4,8},{8,4},{12,0},{1,13},{5,9},{9,5},{13,1},{2,14},{6,10},... | collective-permute-start | bytes 1191944 | tf_op jit(solution)/shard_map/ppermute | solution.py:313
  13.2 104.4 %collective-permute-start.10 = (f32[768,128]{1,0:T(8,128)}, f32[768,128]{1,0:T(8,128)S(1)}, u32[]{:S(2)}, u32[]{:S(2)}) collective-permute-start(f32[768,128]{1,0:T(8,128)} %pack.21), channel_id=1, source_target_pairs={{0,8},{4,12},{8,0},{12,4},{1,9},{5,13},{9,1},{13,5},{2,10},{6,14},... | collective-permute-start | bytes 1179656 | tf_op jit(solution)/shard_map/ppermute | solution.py:313
  17.0 101.1 %collective-permute-start.11 = (f32[768,128]{1,0:T(8,128)}, f32[768,128]{1,0:T(8,128)}, u32[]{:S(2)}, u32[]{:S(2)}) collective-permute-start(f32[768,128]{1,0:T(8,128)} %pack.22), channel_id=1, source_target_pairs={{0,4},{4,0},{8,12},{12,8},{1,5},{5,1},{9,13},{13,9},{2,6},{6,2},{1... | collective-permute-start | bytes 1179656 | tf_op jit(solution)/shard_map/ppermute | solution.py:313
  30.5 2.1 %copy-start.3 = (f32[768,128]{1,0:T(8,128)S(1)}, f32[768,128]{1,0:T(8,128)}, u32[]{:S(2)}) copy-start(f32[768,128]{1,0:T(8,128)} %pack.16) | copy-start | bytes 1179652
  30.5 15.0 %copy-start.2 = (f32[768,128]{1,0:T(8,128)S(1)}, f32[768,128]{1,0:T(8,128)}, u32[]{:S(2)}) copy-start(f32[768,128]{1,0:T(8,128)} %pack.17) | copy-start | bytes 1179652
  30.6 15.0 %copy-start.1 = (f32[768,128]{1,0:T(8,128)S(1)}, f32[768,128]{1,0:T(8,128)}, u32[]{:S(2)}) copy-start(f32[768,128]{1,0:T(8,128)} %pack.18) | copy-start | bytes 1179652
  30.6 40.9 %copy-start.7 = (s32[256]{0:T(256)S(1)}, s32[256]{0:T(256)}, u32[]{:S(2)}) copy-start(s32[256]{0:T(256)} %param.7) | copy-start | bytes 3076
  30.6 42.0 %copy-start = (f32[768,128]{1,0:T(8,128)S(1)}, f32[768,128]{1,0:T(8,128)}, u32[]{:S(2)}) copy-start(f32[768,128]{1,0:T(8,128)} %pack.20) | copy-start | bytes 1179652
  32.6 42.4 %copy-start.9 = (f32[776,128]{1,0:T(8,128)}, f32[776,128]{1,0:T(8,128)S(1)}, u32[]{:S(2)}) copy-start(f32[776,128]{1,0:T(8,128)S(1)} %collective-permute-done.2.refs_2_) | copy-start | bytes 1191940
  32.6 40.0 %collective-permute-start.6 = (f32[768,128]{1,0:T(8,128)S(1)}, f32[768,128]{1,0:T(8,128)}, u32[]{:S(2)}, u32[]{:S(2)}) collective-permute-start(f32[768,128]{1,0:T(8,128)S(1)} %copy-done.3), channel_id=1, source_target_pairs={{0,12},{4,8},{8,4},{12,0},{1,13},{5,9},{9,5},{13,1},{2,14},{6,10},... | collective-permute-start | bytes 1179656 | tf_op jit(solution)/shard_map/ppermute | solution.py:313
  45.6 29.5 %copy-start.10 = (f32[776,128]{1,0:T(8,128)}, f32[776,128]{1,0:T(8,128)S(1)}, u32[]{:S(2)}) copy-start(f32[776,128]{1,0:T(8,128)S(1)} %collective-permute-done.1.refs_1_) | copy-start | bytes 1191940
  45.6 59.2 %collective-permute-start.7 = (f32[768,128]{1,0:T(8,128)S(1)}, f32[768,128]{1,0:T(8,128)}, u32[]{:S(2)}, u32[]{:S(2)}) collective-permute-start(f32[768,128]{1,0:T(8,128)S(1)} %copy-done.2), channel_id=1, source_target_pairs={{0,8},{4,12},{8,0},{12,4},{1,9},{5,13},{9,1},{13,5},{2,10},{6,14},... | collective-permute-start | bytes 1179656 | tf_op jit(solution)/shard_map/ppermute | solution.py:313
  45.6 29.4 %copy-start.11 = (f32[776,128]{1,0:T(8,128)}, f32[776,128]{1,0:T(8,128)S(1)}, u32[]{:S(2)}) copy-start(f32[776,128]{1,0:T(8,128)S(1)} %collective-permute-done.refs_0_) | copy-start | bytes 1191940
  45.6 61.6 %collective-permute-start.8 = (f32[768,128]{1,0:T(8,128)S(1)}, f32[768,128]{1,0:T(8,128)}, u32[]{:S(2)}, u32[]{:S(2)}) collective-permute-start(f32[768,128]{1,0:T(8,128)S(1)} %copy-done.1), channel_id=1, source_target_pairs={{0,4},{4,0},{8,12},{12,8},{1,5},{5,1},{9,13},{13,9},{2,6},{6,2},{1... | collective-permute-start | bytes 1179656 | tf_op jit(solution)/shard_map/ppermute | solution.py:313
  71.5 3.5 %copy-start.8 = (s32[1024]{0:T(1024)}, s32[1024]{0:T(1024)S(1)}, u32[]{:S(2)}) copy-start(s32[1024]{0:T(1024)S(1)} %pad_add_fusion) | copy-start | bytes 12292
  72.6 47.2 %collective-permute-start.9 = (f32[768,128]{1,0:T(8,128)S(1)}, f32[768,128]{1,0:T(8,128)S(1)}, u32[]{:S(2)}, u32[]{:S(2)}) collective-permute-start(f32[768,128]{1,0:T(8,128)S(1)} %copy-done), channel_id=1, source_target_pairs={{0,12},{4,8},{8,4},{12,0},{1,13},{5,9},{9,5},{13,1},{2,14},{6,10},... | collective-permute-start | bytes 1179656 | tf_op jit(solution)/shard_map/ppermute | solution.py:313
  104.8 25.0 %collective-permute-start.3 = (f32[256,128]{1,0:T(8,128)}, f32[256,128]{1,0:T(8,128)S(1)}, u32[]{:S(2)}, u32[]{:S(2)}) collective-permute-start(f32[256,128]{1,0:T(8,128)} %get-tuple-element.18), channel_id=1, source_target_pairs={{0,12},{4,8},{8,4},{12,0},{1,13},{5,9},{9,5},{13,1},{2,14},{6,10},... | collective-permute-start | bytes 393224 | tf_op jit(solution)/shard_map/ppermute | solution.py:313
  107.3 10.4 %copy-start.16 = (f32[256,128]{1,0:T(8,128)S(1)}, f32[256,128]{1,0:T(8,128)}, u32[]{:S(2)}) copy-start(f32[256,128]{1,0:T(8,128)} %get-tuple-element.20) | copy-start | bytes 393220
  107.3 23.5 %collective-permute-start.4 = (f32[256,128]{1,0:T(8,128)}, f32[256,128]{1,0:T(8,128)S(1)}, u32[]{:S(2)}, u32[]{:S(2)}) collective-permute-start(f32[256,128]{1,0:T(8,128)} %get-tuple-element.19), channel_id=1, source_target_pairs={{0,8},{4,12},{8,0},{12,4},{1,9},{5,13},{9,1},{13,5},{2,10},{6,14},... | collective-permute-start | bytes 393224 | tf_op jit(solution)/shard_map/ppermute | solution.py:313
  117.6 3.5 %copy-start.12 = (f32[768,128]{1,0:T(8,128)}, f32[768,128]{1,0:T(8,128)S(1)}, u32[]{:S(2)}) copy-start(f32[768,128]{1,0:T(8,128)S(1)} %collective-permute-done.10.refs_1_) | copy-start | bytes 1179652
  117.6 15.3 %collective-permute-start.5 = (f32[256,128]{1,0:T(8,128)S(1)}, f32[256,128]{1,0:T(8,128)S(1)}, u32[]{:S(2)}, u32[]{:S(2)}) collective-permute-start(f32[256,128]{1,0:T(8,128)S(1)} %copy-done.16), channel_id=1, source_target_pairs={{0,4},{4,0},{8,12},{12,8},{1,5},{5,1},{9,13},{13,9},{2,6},{6,2},{1... | collective-permute-start | bytes 393224 | tf_op jit(solution)/shard_map/ppermute | solution.py:313
  118.1 18.3 %collective-permute-start.12 = (f32[256,128]{1,0:T(8,128)}, f32[256,128]{1,0:T(8,128)S(1)}, u32[]{:S(2)}, u32[]{:S(2)}) collective-permute-start(f32[256,128]{1,0:T(8,128)} %get-tuple-element.23), channel_id=1, source_target_pairs={{0,4},{4,0},{8,12},{12,8},{1,5},{5,1},{9,13},{13,9},{2,6},{6,2},{1... | collective-permute-start | bytes 393224 | tf_op jit(solution)/shard_map/ppermute | solution.py:313
  119.7 1.4 copy-start.13
  119.7 10.1 %copy-start.14 = (f32[256,128]{1,0:T(8,128)S(1)}, f32[256,128]{1,0:T(8,128)}, u32[]{:S(2)}) copy-start(f32[256,128]{1,0:T(8,128)} %get-tuple-element.25) | copy-start | bytes 393220
  119.7 17.7 %collective-permute-start.13 = (f32[256,128]{1,0:T(8,128)}, f32[256,128]{1,0:T(8,128)S(1)}, u32[]{:S(2)}, u32[]{:S(2)}) collective-permute-start(f32[256,128]{1,0:T(8,128)} %get-tuple-element.24), channel_id=1, source_target_pairs={{0,12},{4,8},{8,4},{12,0},{1,13},{5,9},{9,5},{13,1},{2,14},{6,10},... | collective-permute-start | bytes 393224 | tf_op jit(solution)/shard_map/ppermute | solution.py:313
  129.8 6.6 %copy-start.15 = (f32[256,128]{1,0:T(8,128)S(1)}, f32[256,128]{1,0:T(8,128)}, u32[]{:S(2)}) copy-start(f32[256,128]{1,0:T(8,128)} %get-tuple-element.28) | copy-start | bytes 393220
  129.8 4.5 %copy-start.4 = (f32[256,128]{1,0:T(8,128)}, f32[256,128]{1,0:T(8,128)S(1)}, u32[]{:S(2)}) copy-start(f32[256,128]{1,0:T(8,128)S(1)} %collective-permute-done.3.refs_1_) | copy-start | bytes 393220
  129.8 13.0 %collective-permute-start.14 = (f32[256,128]{1,0:T(8,128)S(1)}, f32[256,128]{1,0:T(8,128)S(1)}, u32[]{:S(2)}, u32[]{:S(2)}) collective-permute-start(f32[256,128]{1,0:T(8,128)S(1)} %copy-done.14), channel_id=1, source_target_pairs={{0,8},{4,12},{8,0},{12,4},{1,9},{5,13},{9,1},{13,5},{2,10},{6,14},... | collective-permute-start | bytes 393224 | tf_op jit(solution)/shard_map/ppermute | solution.py:313
  130.7 3.6 %copy-start.5 = (f32[256,128]{1,0:T(8,128)}, f32[256,128]{1,0:T(8,128)S(1)}, u32[]{:S(2)}) copy-start(f32[256,128]{1,0:T(8,128)S(1)} %collective-permute-done.4.refs_2_) | copy-start | bytes 393220
  130.8 12.7 %collective-permute-start.15 = (f32[256,128]{1,0:T(8,128)}, f32[256,128]{1,0:T(8,128)S(1)}, u32[]{:S(2)}, u32[]{:S(2)}) collective-permute-start(f32[256,128]{1,0:T(8,128)} %get-tuple-element.26), channel_id=1, source_target_pairs={{0,4},{4,0},{8,12},{12,8},{1,5},{5,1},{9,13},{13,9},{2,6},{6,2},{1... | collective-permute-start | bytes 393224 | tf_op jit(solution)/shard_map/ppermute | solution.py:313
  133.0 1.4 copy-start.6
  133.0 11.2 %collective-permute-start.16 = (f32[256,128]{1,0:T(8,128)}, f32[256,128]{1,0:T(8,128)S(1)}, u32[]{:S(2)}, u32[]{:S(2)}) collective-permute-start(f32[256,128]{1,0:T(8,128)} %get-tuple-element.27), channel_id=1, source_target_pairs={{0,12},{4,8},{8,4},{12,0},{1,13},{5,9},{9,5},{13,1},{2,14},{6,10},... | collective-permute-start | bytes 393224 | tf_op jit(solution)/shard_map/ppermute | solution.py:313
  136.5 9.7 %collective-permute-start.17 = (f32[256,128]{1,0:T(8,128)S(1)}, f32[256,128]{1,0:T(8,128)S(1)}, u32[]{:S(2)}, u32[]{:S(2)}) collective-permute-start(f32[256,128]{1,0:T(8,128)S(1)} %copy-done.15), channel_id=1, source_target_pairs={{0,8},{4,12},{8,0},{12,4},{1,9},{5,13},{9,1},{13,5},{2,10},{6,14},... | collective-permute-start | bytes 393224 | tf_op jit(solution)/shard_map/ppermute | solution.py:313
